TPU v7x, 32 devices: a whole 2x2x4 slice. The times are simulated.
32 devices in a mesh: row: 4 (over y, x), col: 8 (over z, core).
Axes of the slice: x: 2, y: 2, z: 4, core: 2. Of those that a mesh axis runs over, the one named last changes fastest.
Arguments:
- matrix: float32 [256, 40960], P('row', 'col'), as said below
- pivots: int32 [256], replicated, may hold values from 0 to 255, as said below
- check_weights: float32 [2, 256], P(None, 'row'), may hold values from -0.375 to 0.375
- checksum: float32 [2, 40960], P(None, 'col'), may hold values from -6 to 6
- coefficients: float32 [4, 8], P('row', 'col'), may hold values from 0.125 to 0.5
- checkpoints: int32 [4, 2], P('row'), may hold values from 0 to 3, as said below
Outputs:
- updated: float32 [256, 40960], P('row', 'col')
- new_checksum: float32 [2, 40960], P(None, 'col')
- parity: float32 [256, 40960], P('row', 'col')
Inputs may be any that keep to these rules, and one draw needn't show every extreme that they name: `pivots`: 256 distinct row numbers. `checkpoints`: row index 0 keeps both codes on member 4 - 1, row index 1 on member 0. `matrix`: the first 256 columns are the panel's multipliers, of size about 256 ** -0.5.
All inputs are finite; a program needn't handle non-finite values.
Results may differ from a plain program's by a relative error of at most 0.000098.
Values sent between devices are 32-bit elements; how exact they have to be, the bound alone decides.
No kernel may reach another device: no remote copies, remote signals or barrier semaphores. Data moves between devices by JAX's collectives and lax.ppermute only.
A program may use at most 64 MiB of HBM per device.

v0:
```python
import jax
import jax.numpy as jnp
from jax import lax
from jax.experimental import pallas as pl
from jax.experimental.pallas import tpu as pltpu
from jax.sharding import PartitionSpec as P


CUTS = (0, 1, 3, 4)
LANES = 128
GRANT = 8 << 20
ROOM = 67_043_328


VMEM = pl.BlockSpec(memory_space=pltpu.VMEM)
SMEM = pl.BlockSpec(memory_space=pltpu.SMEM)
HBM = pl.BlockSpec(memory_space=pltpu.HBM)


def near(value):
    return pltpu.with_memory_space_constraint(value, pltpu.VMEM)


def swap(value, axis, mask):
    return lax.ppermute(value, axis, [(i, i ^ mask) for i in range(lax.axis_size(axis))])


def span(bits):
    masks = [0]
    for bit in bits:
        masks += [mask | 1 << bit for mask in masks]
    return masks


def bits_of(count):
    return list(range(count.bit_length() - 1))


def plans_of(n_row):
    bits = bits_of(n_row)
    cut = len(bits) // 2
    return [(bits[:cut], bits[cut:]), (bits[cut:], bits[:cut])]


def panel_stages(n_col):
    bits = bits_of(n_col)[1:]
    stages = [bits[i : i + 2] for i in range(0, len(bits), 2)]
    return stages[::-1] + [[0]]


def call(
    kernel, shapes, in_specs, operands, scratch=(), places=None, aliases=None, flops=0, grant=GRANT
):
    places = places or [VMEM] * len(shapes)
    outs = [
        pltpu.VMEM(shape, jnp.float32) if place is VMEM else jax.ShapeDtypeStruct(shape, jnp.float32)
        for shape, place in zip(shapes, places)
    ]
    operands = [near(x) if spec is VMEM else x for x, spec in zip(operands, in_specs)]
    return pl.pallas_call(
        kernel,
        out_shape=outs,
        in_specs=in_specs,
        out_specs=places,
        scratch_shapes=list(scratch),
        input_output_aliases=aliases or {},
        compiler_params=pltpu.CompilerParams(vmem_limit_bytes=grant),
        cost_estimate=pl.CostEstimate(flops=flops, bytes_accessed=0, transcendentals=0),
    )(*operands)


def prepare(matrix, scale, groups, cuts, width):
    rows, cols = matrix.shape
    half = cols // 2
    sizes = [high - low for low, high in zip(cuts, cuts[1:])]

    def kernel(matrix_ref, scale_ref, *refs):
        sides, panel_ref, parts, sems = refs[:2], refs[2], refs[3:-1], refs[-1]
        copies = []
        for number, (low, high) in enumerate(zip(cuts, cuts[1:])):
            for side in range(2):
                copies.append(
                    pltpu.make_async_copy(
                        matrix_ref.at[low:high, side * half : (side + 1) * half],
                        sides[side].at[low:high, :],
                        sems.at[number, side],
                    )
                )
        for copy in copies:
            copy.start()
        scale = scale_ref[0, 0]
        upper = lax.axis_index("col") // groups & 1
        for number, (low, high) in enumerate(zip(cuts, cuts[1:])):
            size = (high - low) // 2
            for side in range(2):
                copies[2 * number + side].wait()
                there = slice(side * half, (side + 1) * half)
                for part in range(2):
                    other = 1 - upper if part == 0 else upper
                    start = pl.multiple_of(low + size * other, 8)
                    parts[2 * number + part][:, there] = (
                        sides[side][pl.ds(start, size), :] * scale
                    )
        panel_ref[...] = sides[0][:, :width]

    shapes = [(rows, half)] * 2 + [(rows, width)]
    for size in sizes:
        shapes += [(size // 2, cols)] * 2
    outs = call(
        kernel,
        shapes,
        [HBM, SMEM],
        [matrix, scale],
        scratch=[pltpu.SemaphoreType.DMA((len(sizes), 2))],
        grant=ROOM - 4 * (2 * rows * cols + rows * width) - (1 << 19),
    )
    parts = [(outs[3 + 2 * i], outs[4 + 2 * i]) for i in range(len(sizes))]
    return outs[:2], outs[2], parts


def choose(held, arrived, period, masks):
    def kernel(held_ref, *refs):
        digit = lax.axis_index("col") % period
        value = held_ref[...]
        for mask, ref in zip(masks, refs[:-1]):
            value = jnp.where(digit == mask, ref[...], value)
        refs[-1][...] = value

    specs = [VMEM] * (1 + len(arrived))
    return call(kernel, [held.shape], specs, [held, *arrived])[0]


def weigh(held, arrived, period, masks, check_weights):
    rows, width = held.shape
    checks = check_weights.shape[0]

    def kernel(weights_ref, held_ref, *refs):
        digit = lax.axis_index("col") % period
        value = held_ref[...]
        for mask, ref in zip(masks, refs[:-1]):
            value = jnp.where(digit == mask, ref[...], value)
        out_ref = refs[-1]
        out_ref[:rows] = value
        w1, w2, w3 = split(weights_ref[...], 3)
        p1, p2, p3 = split(value, 3)
        left = jnp.concatenate([w1, w1, w2, w2, w1, w3], axis=1)
        right = jnp.concatenate([p1, p2, p1, p2, p3, p1], axis=0)
        out_ref[rows:] = jnp.zeros((8, width), jnp.float32)
        out_ref[rows : rows + checks] = jnp.dot(left, right, preferred_element_type=jnp.float32)

    specs = [VMEM] * (2 + len(arrived))
    operands = [check_weights, held, *arrived]
    return call(kernel, [(rows + 8, width)], specs, operands)[0]


def fold(message, arrived):
    rows = message.shape[0] - 8

    def kernel(message_ref, *refs):
        refs[-1][:rows] = message_ref[:rows]
        total = message_ref[rows:]
        for ref in refs[:-1]:
            total = total + ref[rows:]
        refs[-1][rows:] = total

    return call(kernel, [message.shape], [VMEM] * (1 + len(arrived)), [message, *arrived])[0]


def add(a, b):
    def kernel(a_ref, b_ref, out_ref):
        out_ref[...] = a_ref[...] + b_ref[...]

    return call(kernel, [a.shape], [VMEM, VMEM], [a, b])[0]


def split(value, terms):
    pieces = []
    for _ in range(terms):
        piece = value.astype(jnp.bfloat16)
        value = value - piece.astype(jnp.float32)
        pieces.append(piece)
    return pieces


def multiply(masks, pivots, lefts, sums, blocks, checks):
    width = pivots.shape[1]
    rows, half = blocks[0].shape
    targets = len(lefts)
    depth = len(blocks) * rows
    step = half // max(1, half // 640)

    def kernel(pivots_ref, *refs):
        left_refs, refs = refs[:targets], refs[targets:]
        sum_refs, refs = refs[: len(sums)], refs[len(sums) :]
        block_refs, out_refs = refs[: len(blocks)], refs[len(blocks) :]
        row = lax.broadcasted_iota(jnp.int32, (rows, width), 0)
        own = lax.axis_index("row")
        selector = jnp.concatenate(
            [
                jnp.where(pivots_ref[...] == row + (own ^ mask) * rows, 1.0, 0.0)
                for mask in masks
            ],
            axis=0,
        ).astype(jnp.bfloat16)
        total = sum_refs[0][rows:]
        for ref in sum_refs[1:]:
            total = total + ref[rows:]
        stack = jnp.concatenate([ref[:rows] for ref in left_refs] + [total], axis=0)
        l1, l2 = [
            lax.dot_general(
                piece, selector, (((1,), (1,)), ((), ())), preferred_element_type=jnp.float32
            ).astype(jnp.bfloat16)
            for piece in split(stack, 2)
        ]
        left = jnp.concatenate([l1, l1, l2], axis=1)
        for out_ref in out_refs:
            out_ref[:, half:] = jnp.zeros((rows, LANES), jnp.float32)
        for low in range(0, half, step):
            there = slice(low, low + step)
            x1, x2 = split(jnp.concatenate([ref[:, there] for ref in block_refs], axis=0), 2)
            right = jnp.concatenate([x1, x2, x1], axis=0)
            product = jnp.dot(left, right, preferred_element_type=jnp.float32)
            for k, out_ref in enumerate(out_refs):
                out_ref[:, there] = product[k * rows : (k + 1) * rows]
                for at in range(0, step, LANES):
                    row = (low + at) // LANES * checks
                    out_ref[row : row + checks, half:] = product[
                        targets * rows : targets * rows + checks, at : at + LANES
                    ]

    return call(
        kernel,
        [(rows, half + LANES)] * targets,
        [VMEM] * (1 + targets + len(sums) + len(blocks)),
        [pivots, *lefts, *sums, *blocks],
        flops=2 * (targets * rows + 8) * depth * half,
    )


def subtract(number, matrix, checksum, width, kept, arrived, before):
    rows, half = matrix.shape
    checks, cols = checksum.shape
    pieces = 4

    def kernel(matrix_ref, checksum_ref, kept_ref, arrived_ref, *refs):
        updated_ref, sums_ref, block, line, sems = refs[-5:]
        there = slice(number * half, (number + 1) * half)
        lane = lax.broadcasted_iota(jnp.int32, (1, half), 1)
        live = lane + (lax.axis_index("col") * cols + number * half) >= width
        copies = []
        for k in range(pieces):
            low, high = k * rows // pieces, (k + 1) * rows // pieces
            product = kept_ref[low:high, :half] + arrived_ref[low:high, :half]
            block[low:high, :] = matrix_ref[low:high, :] - jnp.where(live, product, 0.0)
            copies.append(
                pltpu.make_async_copy(
                    block.at[low:high, :], updated_ref.at[low:high, there], sems.at[k]
                )
            )
            copies[-1].start()
        total = kept_ref[:, half:] + arrived_ref[:, half:]
        for at in range(0, half, LANES):
            row = at // LANES * checks
            line[:, at : at + LANES] = checksum_ref[
                :, number * half + at : number * half + at + LANES
            ] - jnp.where(live[:, at : at + LANES], total[row : row + checks], 0.0)
        copies.append(pltpu.make_async_copy(line, sums_ref.at[:, there], sems.at[pieces]))
        copies[-1].start()
        for copy in copies:
            copy.wait()

    return call(
        kernel,
        [(rows, cols), (checks, cols)],
        [VMEM] * 4 + [HBM] * len(before),
        [matrix, checksum, kept, arrived, *before],
        scratch=[
            pltpu.VMEM((rows, half), jnp.float32),
            pltpu.VMEM((checks, half), jnp.float32),
            pltpu.SemaphoreType.DMA((pieces + 1,)),
        ],
        places=[HBM, HBM],
        aliases={4 + i: i for i in range(len(before))},
    )


def store_code(checkpoints, low, piece, arrived, shape, before):
    size, cols = piece.shape
    groups = checkpoints.shape[1]

    def kernel(points_ref, piece_ref, arrived_ref, *refs):
        out_ref, block, sems = refs[-3:]
        index = lax.axis_index("col")
        position = index // groups
        keeper = points_ref[0, 0]
        for k in range(1, groups):
            keeper = jnp.where(index % groups == k, points_ref[0, k], keeper)
        keep = position == keeper
        upper = position & 1 == 1
        copies = []
        for k in range(2):
            there = slice(k * size, (k + 1) * size)
            mine = upper if k else jnp.logical_not(upper)
            value = jnp.where(mine, piece_ref[...], arrived_ref[...])
            block[there, :] = jnp.where(keep, value, 0.0)
            copies.append(
                pltpu.make_async_copy(
                    block.at[there, :],
                    out_ref.at[low + k * size : low + (k + 1) * size, :],
                    sems.at[k],
                )
            )
            copies[-1].start()
        for copy in copies:
            copy.wait()

    return call(
        kernel,
        [shape],
        [SMEM] + [VMEM] * 2 + [HBM] * len(before),
        [checkpoints, piece, arrived, *before],
        scratch=[
            pltpu.VMEM((2 * size, cols), jnp.float32),
            pltpu.SemaphoreType.DMA((2,)),
        ],
        places=[HBM],
        aliases={3 + i: i for i in range(len(before))},
    )


def halves(own, upper):
    half = own.shape[0] // 2
    first, second = own[:half], own[half:]
    return jnp.where(upper, first, second), jnp.where(upper, second, first)


def group_code(outgoing, kept, stride, position, count):
    bits = bits_of(count)
    for bit in bits[:-1]:
        arrived = swap(outgoing, "col", stride << bit)
        piece = add(kept, arrived)
        if bit + 2 < len(bits):
            outgoing, kept = halves(piece, position >> (bit + 1) & 1 == 1)
    for bit in bits[-1:]:
        arrived = swap(piece, "col", stride << bit)
        piece = add(piece, arrived)
    for bit in reversed(bits[:-1]):
        arrived = swap(piece, "col", stride << bit)
        if bit == 0:
            return piece, arrived
        upper = position >> bit & 1 == 1
        piece = jnp.concatenate(
            [jnp.where(upper, arrived, piece), jnp.where(upper, piece, arrived)], axis=0
        )


def per_device(matrix, pivots, check_weights, checksum, coefficients, checkpoints):
    rows, cols = matrix.shape
    width = pivots.shape[0]
    checks = check_weights.shape[0]
    col_index = lax.axis_index("col")
    n_row = lax.axis_size("row")
    n_col = lax.axis_size("col")
    groups = checkpoints.shape[1]
    plans = plans_of(n_row)

    position = col_index // groups
    cuts = [cut * rows // CUTS[-1] for cut in CUTS]
    sides, lower, parts = prepare(matrix, coefficients, groups, cuts, width)

    gathered = []
    for number, (gather, _) in enumerate(plans):
        blocks = [sides[number]]
        for bit in gather:
            message = blocks[0] if len(blocks) == 1 else jnp.concatenate(blocks, axis=0)
            arrived = swap(message, "row", 1 << bit)
            if len(blocks) == 1:
                blocks.append(arrived)
            else:
                blocks += [arrived[i * rows : (i + 1) * rows] for i in range(len(blocks))]
        gathered.append(blocks)

    stages = panel_stages(n_col)
    for number, bits in enumerate(stages):
        masks = span(bits)[1:]
        period = 1 << min(bits) + len(bits)
        came = []
        for mask in masks:
            route = [(i, i | mask) for i in range(0, n_col, period)]
            came.append(lax.ppermute(lower, "col", route))
        if number < len(stages) - 1:
            lower = choose(lower, came, period, masks)
        else:
            message = weigh(lower, came, period, masks, check_weights)
    panel = {}
    came = []
    for mask in span(plans[1][1])[1:]:
        panel[mask] = swap(message, "row", mask)
        came.append(panel[mask])
    message = fold(message, came)
    panel[0] = message
    sums = [message]
    for mask in span(plans[0][1])[1:]:
        panel[mask] = swap(message, "row", mask)
        sums.append(panel[mask])

    results = ()
    for number, (gather, reduce) in enumerate(plans):
        targets = span(reduce)
        lefts = [panel[mask] for mask in targets]
        outs = multiply(span(gather), pivots[None, :], lefts, sums, gathered[number], checks)
        part = dict(zip(targets, outs))
        for place in range(len(reduce) - 1, -1, -1):
            flip = 1 << reduce[place]
            keep = span(reduce[:place])
            sent = [part[mask | flip] for mask in keep]
            message = sent[0] if len(sent) == 1 else jnp.concatenate(sent, axis=0)
            arrived = swap(message, "row", flip)
            if place:
                part = {
                    mask: part[mask] + arrived[i * rows : (i + 1) * rows]
                    for i, mask in enumerate(keep)
                }
        results = subtract(
            number, sides[number], checksum, width, part[0], arrived, results
        )

    parity = ()
    for chunk, (outgoing, kept) in enumerate(parts):
        piece, arrived = group_code(outgoing, kept, groups, position, n_col // groups)
        parity = store_code(checkpoints, cuts[chunk], piece, arrived, (rows, cols), parity)
    return (*results, *parity)


def solution(mesh):
    in_specs = (
        P("row", "col"),
        P(),
        P(None, "row"),
        P(None, "col"),
        P("row", "col"),
        P("row", None),
    )
    out_specs = (P("row", "col"), P(None, "col"), P("row", "col"))
    return jax.shard_map(
        per_device, mesh=mesh, in_specs=in_specs, out_specs=out_specs, check_vma=False
    )
```

profile of v0, /device:TPU:0, one launch (start us, length us, event | category | flops | bytes accessed | tf_op | source)
XLA Modules:
  0.0 75.0 jit_solution(11256063104080349527)
XLA Ops:
  1.3 2.1 %shard_map.85 = (f32[64,2560]{1,0:T(8,128)S(1)}, f32[64,2560]{1,0:T(8,128)S(1)}, f32[64,256]{1,0:T(8,128)S(1)}, f32[8,5120]{1,0:T(8,128)S(1)}, f32[8,5120]{1,0:T...) custom-call(f32[64,5120]{1,0:T(8,128)} %matrix_ref.1, ...), custom_call_target="tpu_custom_call" | custom-call | tf_op jit(solution)/shard_map/pallas_call | solution.py:60
  3.4 3.0 %collective-permute-start.8 = (f32[64,2560]{1,0:T(8,128)S(1)}, f32[64,2560]{1,0:T(8,128)S(1)}, u32[]{:S(2)}, u32[]{:S(2)}) collective-permute-start(f32[64,2560]{1,0:T(8,128)S(1)} %get-tuple-element.24.refs_4_.matrix_ref), channel_id=1, source_target_pairs={{0,8},{8,0},{16,24},{24,16},{1,9},{9,1},{17,25},{25,17},{2,10},{10... | collective-permute-start | bytes 1966088 | tf_op jit(solution)/shard_map/ppermute | solution.py:25
  6.5 1.5 %collective-permute-start.6 = (f32[64,2560]{1,0:T(8,128)S(1)}, f32[64,2560]{1,0:T(8,128)S(1)}, u32[]{:S(2)}, u32[]{:S(2)}) collective-permute-start(f32[64,2560]{1,0:T(8,128)S(1)} %get-tuple-element.20.refs_4_.matrix_ref), channel_id=1, source_target_pairs={{0,16},{8,24},{16,0},{24,8},{1,17},{9,25},{17,1},{25,9},{2,18},{10... | collective-permute-start | bytes 1966088 | tf_op jit(solution)/shard_map/ppermute | solution.py:25
  8.0 3.5 %collective-permute-start = (f32[64,256]{1,0:T(8,128)S(1)}, f32[64,256]{1,0:T(8,128)S(1)}, u32[]{:S(2)}, u32[]{:S(2)}) collective-permute-start(f32[64,256]{1,0:T(8,128)S(1)} %get-tuple-element.21.held_ref), channel_id=1, source_target_pairs={{0,2},{8,10},{16,18},{24,26}} | collective-permute-start | bytes 196616 | tf_op jit(solution)/shard_map/ppermute | solution.py:390
  11.5 1.7 %collective-permute-start.1 = (f32[64,256]{1,0:T(8,128)S(1)}, f32[64,256]{1,0:T(8,128)S(1)}, u32[]{:S(2)}, u32[]{:S(2)}) collective-permute-start(f32[64,256]{1,0:T(8,128)S(1)} %get-tuple-element.21.held_ref), channel_id=1, source_target_pairs={{0,4},{8,12},{16,20},{24,28}} | collective-permute-start | bytes 196616 | tf_op jit(solution)/shard_map/ppermute | solution.py:390
  13.1 1.7 %collective-permute-start.2 = (f32[64,256]{1,0:T(8,128)S(1)}, f32[64,256]{1,0:T(8,128)S(1)}, u32[]{:S(2)}, u32[]{:S(2)}) collective-permute-start(f32[64,256]{1,0:T(8,128)S(1)} %get-tuple-element.21.held_ref), channel_id=1, source_target_pairs={{0,6},{8,14},{16,22},{24,30}} | collective-permute-start | bytes 196616 | tf_op jit(solution)/shard_map/ppermute | solution.py:390
  14.8 1.6 %collective-permute-start.13 = (f32[16,5120]{1,0:T(8,128)}, f32[16,5120]{1,0:T(8,128)S(1)}, u32[]{:S(2)}, u32[]{:S(2)}) collective-permute-start(f32[16,5120]{1,0:T(8,128)} %get-tuple-element.34), channel_id=1, source_target_pairs={{0,2},{1,3},{2,0},{3,1},{4,6},{5,7},{6,4},{7,5},{8,10},{9,11},{10,... | collective-permute-start | bytes 983048 | tf_op jit(solution)/shard_map/ppermute | solution.py:25
  16.9 1.3 %collective-permute-start.3 = (f32[64,256]{1,0:T(8,128)S(1)}, f32[64,256]{1,0:T(8,128)S(1)}, u32[]{:S(2)}, u32[]{:S(2)}) collective-permute-start(f32[64,256]{1,0:T(8,128)S(1)} %shard_map.86.held_ref), channel_id=1, source_target_pairs={{0,1},{2,3},{4,5},{6,7},{8,9},{10,11},{12,13},{14,15},{16,17},{18,... | collective-permute-start | bytes 196616 | tf_op jit(solution)/shard_map/ppermute | solution.py:390
  18.2 0.9 %collective-permute-done.3.refs_0_ = f32[64,256]{1,0:T(8,128)S(1)} collective-permute-done((f32[64,256]{1,0:T(8,128)S(1)}, f32[64,256]{1,0:T(8,128)S(1)}, u32[]{:S(2)}, u32[]{:S(2)}) %collective-permute-start.3) | collective-permute-done | bytes 65568 | tf_op jit(solution)/shard_map/ppermute | solution.py:390
  19.2 0.5 collective-permute-start.4
  19.8 4.0 %collective-permute-done.4.refs_0_.refs_1_ = f32[72,256]{1,0:T(8,128)S(1)} collective-permute-done((f32[72,256]{1,0:T(8,128)S(1)}, f32[72,256]{1,0:T(8,128)S(1)}, u32[]{:S(2)}, u32[]{:S(2)}) %collective-permute-start.4) | collective-permute-done | bytes 73760 | tf_op jit(solution)/shard_map/ppermute | solution.py:25
  23.8 0.8 %collective-permute-start.5 = (f32[72,256]{1,0:T(8,128)S(1)}, f32[72,256]{1,0:T(8,128)S(1)}, u32[]{:S(2)}, u32[]{:S(2)}) collective-permute-start(f32[72,256]{1,0:T(8,128)S(1)} %shard_map.88.refs_0_.refs_2_), channel_id=1, source_target_pairs={{0,16},{8,24},{16,0},{24,8},{1,17},{9,25},{17,1},{25,9},{2,18},{10... | collective-permute-start | bytes 221192 | tf_op jit(solution)/shard_map/ppermute | solution.py:25
  24.6 3.6 %collective-permute-done.5.refs_3_.refs_1_ = f32[72,256]{1,0:T(8,128)S(1)} collective-permute-done((f32[72,256]{1,0:T(8,128)S(1)}, f32[72,256]{1,0:T(8,128)S(1)}, u32[]{:S(2)}, u32[]{:S(2)}) %collective-permute-start.5) | collective-permute-done | bytes 73760 | tf_op jit(solution)/shard_map/ppermute | solution.py:25
  28.2 0.8 %shard_map.90 = (f32[64,2688]{1,0:T(8,128)S(1)}, f32[64,2688]{1,0:T(8,128)S(1)}) custom-call(s32[1,256]{1,0:T(1,128)S(1)} %bitcast.1, f32[72,256]{1,0:T(8,128)S(1)} %shard_map.88.refs_0_.refs_2_, f32[72,256]{1,0:T(8,128)S(1)} %collective-permute-done.5.refs_3_.refs_1_, f32[72,256]{1,0:T(8,128)S(1)} %shard_map.88.refs_0_.refs_2_, ...), custom_call_target="tpu_custom_call" | custom-call | flops 89128960 | tf_op jit(solution)/shard_map/pallas_call | solution.py:60
  29.0 0.8 %collective-permute-start.9 = (f32[64,2688]{1,0:T(8,128)S(1)}, f32[64,2688]{1,0:T(8,128)S(1)}, u32[]{:S(2)}, u32[]{:S(2)}) collective-permute-start(f32[64,2688]{1,0:T(8,128)S(1)} %get-tuple-element.26), channel_id=1, source_target_pairs={{0,16},{8,24},{16,0},{24,8},{1,17},{9,25},{17,1},{25,9},{2,18},{10... | collective-permute-start | bytes 2064392 | tf_op jit(solution)/shard_map/ppermute | solution.py:25
  29.8 0.8 %shard_map.89 = (f32[64,2688]{1,0:T(8,128)S(1)}, f32[64,2688]{1,0:T(8,128)S(1)}) custom-call(s32[1,256]{1,0:T(1,128)S(1)} %bitcast.2, f32[72,256]{1,0:T(8,128)S(1)} %shard_map.88.refs_0_.refs_2_, f32[72,256]{1,0:T(8,128)S(1)} %collective-permute-done.4.refs_0_.refs_1_, f32[72,256]{1,0:T(8,128)S(1)} %shard_map.88.refs_0_.refs_2_, ...), custom_call_target="tpu_custom_call" | custom-call | flops 89128960 | tf_op jit(solution)/shard_map/pallas_call | solution.py:60
  30.6 1.5 %collective-permute-start.7 = (f32[64,2688]{1,0:T(8,128)S(1)}, f32[64,2688]{1,0:T(8,128)S(1)}, u32[]{:S(2)}, u32[]{:S(2)}) collective-permute-start(f32[64,2688]{1,0:T(8,128)S(1)} %get-tuple-element.23), channel_id=1, source_target_pairs={{0,8},{8,0},{16,24},{24,16},{1,9},{9,1},{17,25},{25,17},{2,10},{10... | collective-permute-start | bytes 2064392 | tf_op jit(solution)/shard_map/ppermute | solution.py:25
  32.2 2.7 %collective-permute-start.14 = (f32[16,5120]{1,0:T(8,128)S(1)}, f32[16,5120]{1,0:T(8,128)S(1)}, u32[]{:S(2)}, u32[]{:S(2)}) collective-permute-start(f32[16,5120]{1,0:T(8,128)S(1)} %shard_map.95.a_ref), channel_id=1, source_target_pairs={{0,4},{1,5},{2,6},{3,7},{4,0},{5,1},{6,2},{7,3},{8,12},{9,13},{10,... | collective-permute-start | bytes 983048 | tf_op jit(solution)/shard_map/ppermute | solution.py:25
  34.9 1.6 %collective-permute-start.16 = (f32[8,5120]{1,0:T(8,128)S(1)}, f32[8,5120]{1,0:T(8,128)S(1)}, u32[]{:S(2)}, u32[]{:S(2)}) collective-permute-start(f32[8,5120]{1,0:T(8,128)S(1)} %get-tuple-element.36), channel_id=1, source_target_pairs={{0,2},{1,3},{2,0},{3,1},{4,6},{5,7},{6,4},{7,5},{8,10},{9,11},{10,... | collective-permute-start | bytes 491528 | tf_op jit(solution)/shard_map/ppermute | solution.py:25
  36.9 9.1 %collective-permute-done.16.b_ref = f32[8,5120]{1,0:T(8,128)S(1)} collective-permute-done((f32[8,5120]{1,0:T(8,128)S(1)}, f32[8,5120]{1,0:T(8,128)S(1)}, u32[]{:S(2)}, u32[]{:S(2)}) %collective-permute-start.16) | collective-permute-done | bytes 163872 | tf_op jit(solution)/shard_map/ppermute | solution.py:25
  46.0 3.0 %collective-permute-start.17 = (f32[8,5120]{1,0:T(8,128)S(1)}, f32[8,5120]{1,0:T(8,128)S(1)}, u32[]{:S(2)}, u32[]{:S(2)}) collective-permute-start(f32[8,5120]{1,0:T(8,128)S(1)} %shard_map.97.a_ref), channel_id=1, source_target_pairs={{0,4},{1,5},{2,6},{3,7},{4,0},{5,1},{6,2},{7,3},{8,12},{9,13},{10,... | collective-permute-start | bytes 491528 | tf_op jit(solution)/shard_map/ppermute | solution.py:25
  49.0 0.5 collective-permute-done.10.b_ref
  49.5 3.0 %collective-permute-start.11 = (f32[8,5120]{1,0:T(8,128)S(1)}, f32[8,5120]{1,0:T(8,128)S(1)}, u32[]{:S(2)}, u32[]{:S(2)}) collective-permute-start(f32[8,5120]{1,0:T(8,128)S(1)} %shard_map.93.a_ref), channel_id=1, source_target_pairs={{0,4},{1,5},{2,6},{3,7},{4,0},{5,1},{6,2},{7,3},{8,12},{9,13},{10,... | collective-permute-start | bytes 491528 | tf_op jit(solution)/shard_map/ppermute | solution.py:25
  52.6 6.8 %collective-permute-done.17.b_ref = f32[8,5120]{1,0:T(8,128)S(1)} collective-permute-done((f32[8,5120]{1,0:T(8,128)S(1)}, f32[8,5120]{1,0:T(8,128)S(1)}, u32[]{:S(2)}, u32[]{:S(2)}) %collective-permute-start.17) | collective-permute-done | bytes 163872 | tf_op jit(solution)/shard_map/ppermute | solution.py:25
  59.6 1.7 %collective-permute-done.11.b_ref = f32[8,5120]{1,0:T(8,128)S(1)} collective-permute-done((f32[8,5120]{1,0:T(8,128)S(1)}, f32[8,5120]{1,0:T(8,128)S(1)}, u32[]{:S(2)}, u32[]{:S(2)}) %collective-permute-start.11) | collective-permute-done | bytes 163872 | tf_op jit(solution)/shard_map/ppermute | solution.py:25
  61.2 0.6 collective-permute-start.12
  61.9 7.1 %collective-permute-done.18.arrived_ref = f32[8,5120]{1,0:T(8,128)S(1)} collective-permute-done((f32[8,5120]{1,0:T(8,128)S(1)}, f32[8,5120]{1,0:T(8,128)S(1)}, u32[]{:S(2)}, u32[]{:S(2)}) %collective-permute-start.18) | collective-permute-done | bytes 163872 | tf_op jit(solution)/shard_map/ppermute | solution.py:25
  69.0 1.3 %shard_map.99.refs_0_ = f32[64,5120]{1,0:T(8,128)} custom-call(s32[1,2]{1,0:T(1,128)S(1)} %copy-done.1, f32[8,5120]{1,0:T(8,128)S(1)} %shard_map.98.piece_ref, f32[8,5120]{1,0:T(8,128)S(1)} %collective-permute-done.18.arrived_ref), custom_call_target="tpu_custom_call" | custom-call | tf_op jit(solution)/shard_map/pallas_call | solution.py:60
  70.3 1.5 %shard_map.100.refs_0_ = f32[64,5120]{1,0:T(8,128)} custom-call(s32[1,2]{1,0:T(1,128)S(1)} %copy-done.1, f32[16,5120]{1,0:T(8,128)S(1)} %shard_map.96.piece_ref, f32[16,5120]{1,0:T(8,128)S(1)} %collective-permute-done.15.arrived_ref, f32[64,5120]{1,0:T(8,128)} %shard_map.99.refs_0_), custom_call_target="tpu_custom_call", output_to_operand_aliasing={{}: (3, {})} | custom-call | tf_op jit(solution)/shard_map/pallas_call | solution.py:60
  71.8 1.3 %shard_map.101 = f32[64,5120]{1,0:T(8,128)} custom-call(s32[1,2]{1,0:T(1,128)S(1)} %copy-done.1, f32[8,5120]{1,0:T(8,128)S(1)} %shard_map.94.piece_ref, f32[8,5120]{1,0:T(8,128)S(1)} %collective-permute-done.12.arrived_ref, f32[64,5120]{1,0:T(8,128)} %shard_map.100.refs_0_), custom_call_target="tpu_custom_call", output_to_operand_aliasing={{}: (3, {})} | custom-call | tf_op jit(solution)/shard_map/pallas_call | solution.py:60
  73.2 0.9 %shard_map.91 = (f32[64,5120]{1,0:T(8,128)}, f32[2,5120]{1,0:T(2,128)}) custom-call(f32[64,2560]{1,0:T(8,128)S(1)} %get-tuple-element.24.refs_4_.matrix_ref, f32[2,5120]{1,0:T(2,128)S(1)} %copy-done, f32[64,2688]{1,0:T(8,128)S(1)} %get-tuple-element.25.kept_ref, f32[64,2688]{1,0:T(8,128)S(1)} %collective-permute-done.9.arrived_ref), custom_call_target="tpu_custom_call" | custom-call | tf_op jit(solution)/shard_map/pallas_call | solution.py:60
  74.1 0.9 %shard_map.92 = (f32[64,5120]{1,0:T(8,128)}, f32[2,5120]{1,0:T(2,128)}) custom-call(f32[64,2560]{1,0:T(8,128)S(1)} %get-tuple-element.20.refs_4_.matrix_ref, f32[2,5120]{1,0:T(2,128)S(1)} %copy-done, f32[64,2688]{1,0:T(8,128)S(1)} %get-tuple-element.22.kept_ref, ...), custom_call_target="tpu_custom_call", output_to_operand_aliasing={{0}: (4, {}), {1}: (5, {})} | custom-call | tf_op jit(solution)/shard_map/pallas_call | solution.py:60
  (31 shorter events, 1.5 us)
Async XLA Ops:
  0.6 18.4 %copy-start.3 = (f32[2,64]{1,0:T(2,128)S(1)}, f32[2,64]{1,0:T(2,128)}, u32[]{:S(2)}) copy-start(f32[2,64]{1,0:T(2,128)} %weights_ref.1) | copy-start | bytes 1540
  0.6 27.6 %copy-start.2 = (s32[256]{0:T(256)S(1)}, s32[256]{0:T(256)}, u32[]{:S(2)}) copy-start(s32[256]{0:T(256)} %param.7) | copy-start | bytes 3076
  3.4 24.8 %collective-permute-start.8 = (f32[64,2560]{1,0:T(8,128)S(1)}, f32[64,2560]{1,0:T(8,128)S(1)}, u32[]{:S(2)}, u32[]{:S(2)}) collective-permute-start(f32[64,2560]{1,0:T(8,128)S(1)} %get-tuple-element.24.refs_4_.matrix_ref), channel_id=1, source_target_pairs={{0,8},{8,0},{16,24},{24,16},{1,9},{9,1},{17,25},{25,17},{2,10},{10... | collective-permute-start | bytes 1966088 | tf_op jit(solution)/shard_map/ppermute | solution.py:25
  6.5 23.4 %collective-permute-start.6 = (f32[64,2560]{1,0:T(8,128)S(1)}, f32[64,2560]{1,0:T(8,128)S(1)}, u32[]{:S(2)}, u32[]{:S(2)}) collective-permute-start(f32[64,2560]{1,0:T(8,128)S(1)} %get-tuple-element.20.refs_4_.matrix_ref), channel_id=1, source_target_pairs={{0,16},{8,24},{16,0},{24,8},{1,17},{9,25},{17,1},{25,9},{2,18},{10... | collective-permute-start | bytes 1966088 | tf_op jit(solution)/shard_map/ppermute | solution.py:25
  8.0 6.9 %collective-permute-start = (f32[64,256]{1,0:T(8,128)S(1)}, f32[64,256]{1,0:T(8,128)S(1)}, u32[]{:S(2)}, u32[]{:S(2)}) collective-permute-start(f32[64,256]{1,0:T(8,128)S(1)} %get-tuple-element.21.held_ref), channel_id=1, source_target_pairs={{0,2},{8,10},{16,18},{24,26}} | collective-permute-start | bytes 196616 | tf_op jit(solution)/shard_map/ppermute | solution.py:390
  11.5 4.9 %collective-permute-start.1 = (f32[64,256]{1,0:T(8,128)S(1)}, f32[64,256]{1,0:T(8,128)S(1)}, u32[]{:S(2)}, u32[]{:S(2)}) collective-permute-start(f32[64,256]{1,0:T(8,128)S(1)} %get-tuple-element.21.held_ref), channel_id=1, source_target_pairs={{0,4},{8,12},{16,20},{24,28}} | collective-permute-start | bytes 196616 | tf_op jit(solution)/shard_map/ppermute | solution.py:390
  13.1 3.7 %collective-permute-start.2 = (f32[64,256]{1,0:T(8,128)S(1)}, f32[64,256]{1,0:T(8,128)S(1)}, u32[]{:S(2)}, u32[]{:S(2)}) collective-permute-start(f32[64,256]{1,0:T(8,128)S(1)} %get-tuple-element.21.held_ref), channel_id=1, source_target_pairs={{0,6},{8,14},{16,22},{24,30}} | collective-permute-start | bytes 196616 | tf_op jit(solution)/shard_map/ppermute | solution.py:390
  14.8 17.3 %collective-permute-start.13 = (f32[16,5120]{1,0:T(8,128)}, f32[16,5120]{1,0:T(8,128)S(1)}, u32[]{:S(2)}, u32[]{:S(2)}) collective-permute-start(f32[16,5120]{1,0:T(8,128)} %get-tuple-element.34), channel_id=1, source_target_pairs={{0,2},{1,3},{2,0},{3,1},{4,6},{5,7},{6,4},{7,5},{8,10},{9,11},{10,... | collective-permute-start | bytes 983048 | tf_op jit(solution)/shard_map/ppermute | solution.py:25
  16.9 2.2 %collective-permute-start.3 = (f32[64,256]{1,0:T(8,128)S(1)}, f32[64,256]{1,0:T(8,128)S(1)}, u32[]{:S(2)}, u32[]{:S(2)}) collective-permute-start(f32[64,256]{1,0:T(8,128)S(1)} %shard_map.86.held_ref), channel_id=1, source_target_pairs={{0,1},{2,3},{4,5},{6,7},{8,9},{10,11},{12,13},{14,15},{16,17},{18,... | collective-permute-start | bytes 196616 | tf_op jit(solution)/shard_map/ppermute | solution.py:390
  19.2 4.5 %collective-permute-start.4 = (f32[72,256]{1,0:T(8,128)S(1)}, f32[72,256]{1,0:T(8,128)S(1)}, u32[]{:S(2)}, u32[]{:S(2)}) collective-permute-start(f32[72,256]{1,0:T(8,128)S(1)} %shard_map.87.message_ref), channel_id=1, source_target_pairs={{0,8},{8,0},{16,24},{24,16},{1,9},{9,1},{17,25},{25,17},{2,10},{10... | collective-permute-start | bytes 221192 | tf_op jit(solution)/shard_map/ppermute | solution.py:25
  23.8 4.4 %collective-permute-start.5 = (f32[72,256]{1,0:T(8,128)S(1)}, f32[72,256]{1,0:T(8,128)S(1)}, u32[]{:S(2)}, u32[]{:S(2)}) collective-permute-start(f32[72,256]{1,0:T(8,128)S(1)} %shard_map.88.refs_0_.refs_2_), channel_id=1, source_target_pairs={{0,16},{8,24},{16,0},{24,8},{1,17},{9,25},{17,1},{25,9},{2,18},{10... | collective-permute-start | bytes 221192 | tf_op jit(solution)/shard_map/ppermute | solution.py:25
  29.0 44.1 %collective-permute-start.9 = (f32[64,2688]{1,0:T(8,128)S(1)}, f32[64,2688]{1,0:T(8,128)S(1)}, u32[]{:S(2)}, u32[]{:S(2)}) collective-permute-start(f32[64,2688]{1,0:T(8,128)S(1)} %get-tuple-element.26), channel_id=1, source_target_pairs={{0,16},{8,24},{16,0},{24,8},{1,17},{9,25},{17,1},{25,9},{2,18},{10... | collective-permute-start | bytes 2064392 | tf_op jit(solution)/shard_map/ppermute | solution.py:25
  30.6 43.5 %collective-permute-start.7 = (f32[64,2688]{1,0:T(8,128)S(1)}, f32[64,2688]{1,0:T(8,128)S(1)}, u32[]{:S(2)}, u32[]{:S(2)}) collective-permute-start(f32[64,2688]{1,0:T(8,128)S(1)} %get-tuple-element.23), channel_id=1, source_target_pairs={{0,8},{8,0},{16,24},{24,16},{1,9},{9,1},{17,25},{25,17},{2,10},{10... | collective-permute-start | bytes 2064392 | tf_op jit(solution)/shard_map/ppermute | solution.py:25
  32.2 20.3 %collective-permute-start.14 = (f32[16,5120]{1,0:T(8,128)S(1)}, f32[16,5120]{1,0:T(8,128)S(1)}, u32[]{:S(2)}, u32[]{:S(2)}) collective-permute-start(f32[16,5120]{1,0:T(8,128)S(1)} %shard_map.95.a_ref), channel_id=1, source_target_pairs={{0,4},{1,5},{2,6},{3,7},{4,0},{5,1},{6,2},{7,3},{8,12},{9,13},{10,... | collective-permute-start | bytes 983048 | tf_op jit(solution)/shard_map/ppermute | solution.py:25
  34.9 11.1 %collective-permute-start.16 = (f32[8,5120]{1,0:T(8,128)S(1)}, f32[8,5120]{1,0:T(8,128)S(1)}, u32[]{:S(2)}, u32[]{:S(2)}) collective-permute-start(f32[8,5120]{1,0:T(8,128)S(1)} %get-tuple-element.36), channel_id=1, source_target_pairs={{0,2},{1,3},{2,0},{3,1},{4,6},{5,7},{6,4},{7,5},{8,10},{9,11},{10,... | collective-permute-start | bytes 491528 | tf_op jit(solution)/shard_map/ppermute | solution.py:25
  36.4 13.0 %collective-permute-start.10 = (f32[8,5120]{1,0:T(8,128)S(1)}, f32[8,5120]{1,0:T(8,128)S(1)}, u32[]{:S(2)}, u32[]{:S(2)}) collective-permute-start(f32[8,5120]{1,0:T(8,128)S(1)} %get-tuple-element.32), channel_id=1, source_target_pairs={{0,2},{1,3},{2,0},{3,1},{4,6},{5,7},{6,4},{7,5},{8,10},{9,11},{10,... | collective-permute-start | bytes 491528 | tf_op jit(solution)/shard_map/ppermute | solution.py:25
  46.0 23.0 %copy-start.1 = (s32[1,2]{1,0:T(1,128)S(1)}, s32[1,2]{1,0:T(1,128)}, u32[]{:S(2)}) copy-start(s32[1,2]{1,0:T(1,128)} %points_ref.5) | copy-start | bytes 28
  46.0 13.5 %collective-permute-start.17 = (f32[8,5120]{1,0:T(8,128)S(1)}, f32[8,5120]{1,0:T(8,128)S(1)}, u32[]{:S(2)}, u32[]{:S(2)}) collective-permute-start(f32[8,5120]{1,0:T(8,128)S(1)} %shard_map.97.a_ref), channel_id=1, source_target_pairs={{0,4},{1,5},{2,6},{3,7},{4,0},{5,1},{6,2},{7,3},{8,12},{9,13},{10,... | collective-permute-start | bytes 491528 | tf_op jit(solution)/shard_map/ppermute | solution.py:25
  49.5 11.7 %collective-permute-start.11 = (f32[8,5120]{1,0:T(8,128)S(1)}, f32[8,5120]{1,0:T(8,128)S(1)}, u32[]{:S(2)}, u32[]{:S(2)}) collective-permute-start(f32[8,5120]{1,0:T(8,128)S(1)} %shard_map.93.a_ref), channel_id=1, source_target_pairs={{0,4},{1,5},{2,6},{3,7},{4,0},{5,1},{6,2},{7,3},{8,12},{9,13},{10,... | collective-permute-start | bytes 491528 | tf_op jit(solution)/shard_map/ppermute | solution.py:25
  52.5 17.8 %collective-permute-start.15 = (f32[16,5120]{1,0:T(8,128)S(1)}, f32[16,5120]{1,0:T(8,128)S(1)}, u32[]{:S(2)}, u32[]{:S(2)}) collective-permute-start(f32[16,5120]{1,0:T(8,128)S(1)} %shard_map.96.piece_ref), channel_id=1, source_target_pairs={{0,2},{1,3},{2,0},{3,1},{4,6},{5,7},{6,4},{7,5},{8,10},{9,11},{10,... | collective-permute-start | bytes 983048 | tf_op jit(solution)/shard_map/ppermute | solution.py:25
  59.5 9.5 %collective-permute-start.18 = (f32[8,5120]{1,0:T(8,128)S(1)}, f32[8,5120]{1,0:T(8,128)S(1)}, u32[]{:S(2)}, u32[]{:S(2)}) collective-permute-start(f32[8,5120]{1,0:T(8,128)S(1)} %shard_map.98.piece_ref), channel_id=1, source_target_pairs={{0,2},{1,3},{2,0},{3,1},{4,6},{5,7},{6,4},{7,5},{8,10},{9,11},{10,... | collective-permute-start | bytes 491528 | tf_op jit(solution)/shard_map/ppermute | solution.py:25
  61.2 10.6 %collective-permute-start.12 = (f32[8,5120]{1,0:T(8,128)S(1)}, f32[8,5120]{1,0:T(8,128)S(1)}, u32[]{:S(2)}, u32[]{:S(2)}) collective-permute-start(f32[8,5120]{1,0:T(8,128)S(1)} %shard_map.94.piece_ref), channel_id=1, source_target_pairs={{0,2},{1,3},{2,0},{3,1},{4,6},{5,7},{6,4},{7,5},{8,10},{9,11},{10,... | collective-permute-start | bytes 491528 | tf_op jit(solution)/shard_map/ppermute | solution.py:25
  71.8 1.4 %copy-start = (f32[2,5120]{1,0:T(2,128)S(1)}, f32[2,5120]{1,0:T(2,128)}, u32[]{:S(2)}) copy-start(f32[2,5120]{1,0:T(2,128)} %checksum_ref.3) | copy-start | bytes 122884
where the time goes:
time: 75.2 us; the launch traced here: 75 us
  waiting for transfers between devices  34.2 us (45%)
  starting transfers between devices  29.3 us (39%)
  Pallas kernels  9.95 us (13%)
  between operations  1.52 us (2%)
    ppermute x15, waiting for transfers between devices, swap(): lax.ppermute(value, axis, [(i, i ^ mask) for i in range(lax.axis_size(axi...  32.9 us
    ppermute x15, starting transfers between devices, swap(): lax.ppermute(value, axis, [(i, i ^ mask) for i in range(lax.axis_size(axi...  21.2 us
    pallas_call x17, Pallas kernels, call(): pl.pallas_call(kernel, out_shape=outs, in_specs=in_specs, out_specs=place...  9.95 us
    ppermute x4, starting transfers between devices, per_device(): came.append(lax.ppermute(lower, 'col', route))  8.12 us
  transfers between devices with their start and end apart: 19, of which 9 were waited for; matrix products, arithmetic and copies ran while one was open for 0% of the time, Pallas kernels for 9%

commit v1 on v0

--- a/solution.py
+++ b/solution.py
@@ -6,7 +6,7 @@
 from jax.sharding import PartitionSpec as P
 
 
-CUTS = (0, 1, 3, 4)
+CUTS = (0, 8, 20, 32, 40)
 LANES = 128
 GRANT = 8 << 20
 ROOM = 67_043_328
@@ -69,58 +69,71 @@
     )(*operands)
 
 
-def prepare(matrix, scale, groups, cuts, width):
+def prepare(matrix, scale, groups, cuts, width, carry):
     rows, cols = matrix.shape
     half = cols // 2
-    sizes = [high - low for low, high in zip(cuts, cuts[1:])]
+    deep = rows // 2
+    count = len(cuts) - 1
+    pieces = 2
+    step = deep // pieces
 
     def kernel(matrix_ref, scale_ref, *refs):
         sides, panel_ref, parts, sems = refs[:2], refs[2], refs[3:-1], refs[-1]
         copies = []
-        for number, (low, high) in enumerate(zip(cuts, cuts[1:])):
+        for piece in range(2 * pieces):
+            lines = slice(piece * step, (piece + 1) * step)
             for side in range(2):
                 copies.append(
                     pltpu.make_async_copy(
-                        matrix_ref.at[low:high, side * half : (side + 1) * half],
-                        sides[side].at[low:high, :],
-                        sems.at[number, side],
+                        matrix_ref.at[lines, side * half : (side + 1) * half],
+                        sides[side].at[lines, :],
+                        sems.at[piece, side],
                     )
                 )
         for copy in copies:
             copy.start()
         scale = scale_ref[0, 0]
         upper = lax.axis_index("col") // groups & 1
-        for number, (low, high) in enumerate(zip(cuts, cuts[1:])):
-            size = (high - low) // 2
+        for copy in copies:
+            copy.wait()
+        for number in range(count):
             for side in range(2):
-                copies[2 * number + side].wait()
-                there = slice(side * half, (side + 1) * half)
-                for part in range(2):
-                    other = 1 - upper if part == 0 else upper
-                    start = pl.multiple_of(low + size * other, 8)
-                    parts[2 * number + part][:, there] = (
-                        sides[side][pl.ds(start, size), :] * scale
-                    )
+                low = max(cuts[number], side * half)
+                high = min(cuts[number + 1], (side + 1) * half)
+                if low < high:
+                    here = slice(low - side * half, high - side * half)
+                    there = slice(low - cuts[number], high - cuts[number])
+                    for part in range(2):
+                        other = 1 - upper if part == 0 else upper
+                        start = pl.multiple_of(deep * other, 8)
+                        parts[2 * number + part][:, there] = (
+                            sides[side][pl.ds(start, deep), here] * scale
+                        )
         panel_ref[...] = sides[0][:, :width]
+        if carry:
+            for k in range(2):
+                there = slice(cuts[1] + k * width, cuts[1] + (k + 1) * width)
+                parts[0][:, there] = sides[0][k * deep : (k + 1) * deep, :width]
 
     shapes = [(rows, half)] * 2 + [(rows, width)]
-    for size in sizes:
-        shapes += [(size // 2, cols)] * 2
+    for number in range(count):
+        size = cuts[number + 1] - cuts[number]
+        shapes += [(deep, size + (2 * width if carry and number == 0 else 0)), (deep, size)]
     outs = call(
         kernel,
         shapes,
         [HBM, SMEM],
         [matrix, scale],
-        scratch=[pltpu.SemaphoreType.DMA((len(sizes), 2))],
-        grant=ROOM - 4 * (2 * rows * cols + rows * width) - (1 << 19),
-    )
-    parts = [(outs[3 + 2 * i], outs[4 + 2 * i]) for i in range(len(sizes))]
+        scratch=[pltpu.SemaphoreType.DMA((2 * pieces, 2))],
+        grant=ROOM - 4 * (2 * rows * cols + 2 * rows * width) - (1 << 19),
+    )
+    parts = [(outs[3 + 2 * i], outs[4 + 2 * i]) for i in range(count)]
     return outs[:2], outs[2], parts
 
 
-def choose(held, arrived, period, masks):
+def choose(held, arrived, field, masks):
     def kernel(held_ref, *refs):
-        digit = lax.axis_index("col") % period
+        digit = lax.axis_index("col") & field
         value = held_ref[...]
         for mask, ref in zip(masks, refs[:-1]):
             value = jnp.where(digit == mask, ref[...], value)
@@ -130,12 +143,12 @@
     return call(kernel, [held.shape], specs, [held, *arrived])[0]
 
 
-def weigh(held, arrived, period, masks, check_weights):
+def weigh(held, arrived, field, masks, check_weights):
     rows, width = held.shape
     checks = check_weights.shape[0]
 
     def kernel(weights_ref, held_ref, *refs):
-        digit = lax.axis_index("col") % period
+        digit = lax.axis_index("col") & field
         value = held_ref[...]
         for mask, ref in zip(masks, refs[:-1]):
             value = jnp.where(digit == mask, ref[...], value)
@@ -171,6 +184,22 @@
         out_ref[...] = a_ref[...] + b_ref[...]
 
     return call(kernel, [a.shape], [VMEM, VMEM], [a, b])[0]
+
+
+def add_and_unpack(kept, arrived, panel, groups):
+    height, cols = kept.shape
+    rows, width = panel.shape
+
+    def kernel(kept_ref, arrived_ref, held_ref, out_ref, panel_ref):
+        out_ref[...] = kept_ref[...] + arrived_ref[:, :cols]
+        came = lax.axis_index("col") // groups & 1 == 1
+        for k in range(rows // height):
+            lines = slice(k * height, (k + 1) * height)
+            there = slice(cols + k * width, cols + (k + 1) * width)
+            panel_ref[lines, :] = jnp.where(came, arrived_ref[:, there], held_ref[lines, :])
+
+    shapes = [kept.shape, panel.shape]
+    return call(kernel, shapes, [VMEM] * 3, [kept, arrived, panel])
 
 
 def split(value, terms):
@@ -306,7 +335,7 @@
             copies.append(
                 pltpu.make_async_copy(
                     block.at[there, :],
-                    out_ref.at[low + k * size : low + (k + 1) * size, :],
+                    out_ref.at[there, low : low + cols],
                     sems.at[k],
                 )
             )
@@ -334,7 +363,7 @@
     return jnp.where(upper, first, second), jnp.where(upper, second, first)
 
 
-def group_code(outgoing, kept, stride, position, count):
+def reduce_code(outgoing, kept, stride, position, count):
     bits = bits_of(count)
     for bit in bits[:-1]:
         arrived = swap(outgoing, "col", stride << bit)
@@ -344,6 +373,11 @@
     for bit in bits[-1:]:
         arrived = swap(piece, "col", stride << bit)
         piece = add(piece, arrived)
+    return piece
+
+
+def gather_code(piece, stride, position, count):
+    bits = bits_of(count)
     for bit in reversed(bits[:-1]):
         arrived = swap(piece, "col", stride << bit)
         if bit == 0:
@@ -365,8 +399,10 @@
     plans = plans_of(n_row)
 
     position = col_index // groups
-    cuts = [cut * rows // CUTS[-1] for cut in CUTS]
-    sides, lower, parts = prepare(matrix, coefficients, groups, cuts, width)
+    cuts = [cut * (cols // LANES) // CUTS[-1] * LANES for cut in CUTS]
+    members = n_col // groups
+    carry = len(bits_of(members)) == 2 and groups == 2
+    sides, lower, parts = prepare(matrix, coefficients, groups, cuts, width, carry)
 
     gathered = []
     for number, (gather, _) in enumerate(plans):
@@ -380,18 +416,31 @@
                 blocks += [arrived[i * rows : (i + 1) * rows] for i in range(len(blocks))]
         gathered.append(blocks)
 
+    codes = []
     stages = panel_stages(n_col)
+    if carry:
+        arrived = swap(parts[0][0], "col", groups)
+        piece, lower = add_and_unpack(parts[0][1], arrived, lower, groups)
+        arrived = swap(piece, "col", 2 * groups)
+        codes.append(add(piece, arrived))
+        stages = [[2], [0]]
     for number, bits in enumerate(stages):
         masks = span(bits)[1:]
         period = 1 << min(bits) + len(bits)
+        starts = range(0, n_col, period)
+        field = period - 1
+        if carry and number == 0:
+            field = masks[0]
         came = []
         for mask in masks:
-            route = [(i, i | mask) for i in range(0, n_col, period)]
+            route = [(i, i | mask) for i in starts]
+            if carry:
+                route = [(i, i ^ mask) for i in range(0, n_col, groups if number == 0 else 1)]
             came.append(lax.ppermute(lower, "col", route))
         if number < len(stages) - 1:
-            lower = choose(lower, came, period, masks)
+            lower = choose(lower, came, field, masks)
         else:
-            message = weigh(lower, came, period, masks, check_weights)
+            message = weigh(lower, came, field, masks, check_weights)
     panel = {}
     came = []
     for mask in span(plans[1][1])[1:]:
@@ -425,9 +474,11 @@
             number, sides[number], checksum, width, part[0], arrived, results
         )
 
+    for chunk in range(len(codes), len(parts)):
+        codes.append(reduce_code(*parts[chunk], groups, position, members))
     parity = ()
-    for chunk, (outgoing, kept) in enumerate(parts):
-        piece, arrived = group_code(outgoing, kept, groups, position, n_col // groups)
+    for chunk, piece in enumerate(codes):
+        piece, arrived = gather_code(piece, groups, position, members)
         parity = store_code(checkpoints, cuts[chunk], piece, arrived, (rows, cols), parity)
     return (*results, *parity)
 

time: 75.2 us -> 84.1 us (1.12)
  waiting for transfers between devices: 34.2 us -> 47.6 us
  starting transfers between devices: 29.3 us -> 24.3 us
    ppermute x15 -> x18, waiting for transfers between devices: 32.9 us -> 43.8 us  [swap(): lax.ppermute(value, axis, [(i, i ^ mask) for i in range(lax.axis_size(axi...]
    ppermute x4 -> x2, starting transfers between devices: 8.12 us -> 4.57 us  [per_device(): came.append(lax.ppermute(lower, 'col', route))]
    ppermute x4 -> x2, waiting for transfers between devices: 1.33 us -> 3.79 us  [per_device(): came.append(lax.ppermute(lower, 'col', route))]
    ppermute x15 -> x18, starting transfers between devices: 21.2 us -> 19.7 us  [swap(): lax.ppermute(value, axis, [(i, i ^ mask) for i in range(lax.axis_size(axi...]
    pallas_call x17 -> x20, Pallas kernels: 9.95 us -> 10.5 us  [call(): pl.pallas_call(kernel, out_shape=outs, in_specs=in_specs, out_specs=place...]
  transfers between devices with their start and end apart: 19 -> 20, of which waited for: 9 -> 15; matrix products, arithmetic and copies ran while one was open for 0% -> 0% of each run, Pallas kernels for 9% -> 10%
where the time goes in v1:
time: 84.1 us; the launch traced here: 83.9 us
  waiting for transfers between devices  47.6 us (57%)
  starting transfers between devices  24.3 us (29%)
  Pallas kernels  10.5 us (12%)
  between operations  1.48 us (2%)
    ppermute x18, waiting for transfers between devices, swap(): lax.ppermute(value, axis, [(i, i ^ mask) for i in range(lax.axis_size(axi...  43.8 us
    ppermute x18, starting transfers between devices, swap(): lax.ppermute(value, axis, [(i, i ^ mask) for i in range(lax.axis_size(axi...  19.7 us
    pallas_call x20, Pallas kernels, call(): pl.pallas_call(kernel, out_shape=outs, in_specs=in_specs, out_specs=place...  10.5 us
    ppermute x2, starting transfers between devices, per_device(): came.append(lax.ppermute(lower, 'col', route))  4.57 us
    ppermute x2, waiting for transfers between devices, per_device(): came.append(lax.ppermute(lower, 'col', route))  3.79 us
  transfers between devices with their start and end apart: 20, of which 15 were waited for; matrix products, arithmetic and copies ran while one was open for 0% of the time, Pallas kernels for 10%

profile of v1, /device:TPU:0, one launch (start us, length us, event | category | flops | bytes accessed | tf_op | source)
XLA Modules:
  0.0 83.9 jit_solution(5461441812553749388)
XLA Ops:
  1.3 1.6 %shard_map.85 = (f32[64,2560]{1,0:T(8,128)S(1)}, f32[64,2560]{1,0:T(8,128)S(1)}, f32[64,256]{1,0:T(8,128)S(1)}, f32[32,1536]{1,0:T(8,128)S(1)}, f32[32,1024]{1,0...) custom-call(f32[64,5120]{1,0:T(8,128)} %matrix_ref.1, ...), custom_call_target="tpu_custom_call" | custom-call | tf_op jit(solution)/shard_map/pallas_call | solution.py:60
  2.9 3.0 %collective-permute-start.7 = (f32[64,2560]{1,0:T(8,128)S(1)}, f32[64,2560]{1,0:T(8,128)S(1)}, u32[]{:S(2)}, u32[]{:S(2)}) collective-permute-start(f32[64,2560]{1,0:T(8,128)S(1)} %get-tuple-element.31.refs_4_.matrix_ref), channel_id=1, source_target_pairs={{0,8},{8,0},{16,24},{24,16},{1,9},{9,1},{17,25},{25,17},{2,10},{10... | collective-permute-start | bytes 1966088 | tf_op jit(solution)/shard_map/ppermute | solution.py:25
  5.9 1.5 %collective-permute-start.5 = (f32[64,2560]{1,0:T(8,128)S(1)}, f32[64,2560]{1,0:T(8,128)S(1)}, u32[]{:S(2)}, u32[]{:S(2)}) collective-permute-start(f32[64,2560]{1,0:T(8,128)S(1)} %get-tuple-element.24.refs_4_.matrix_ref), channel_id=1, source_target_pairs={{0,16},{8,24},{16,0},{24,8},{1,17},{9,25},{17,1},{25,9},{2,18},{10... | collective-permute-start | bytes 1966088 | tf_op jit(solution)/shard_map/ppermute | solution.py:25
  7.4 1.6 %collective-permute-start = (f32[32,1536]{1,0:T(8,128)S(1)}, f32[32,1536]{1,0:T(8,128)S(1)}, u32[]{:S(2)}, u32[]{:S(2)}) collective-permute-start(f32[32,1536]{1,0:T(8,128)S(1)} %get-tuple-element.26), channel_id=1, source_target_pairs={{0,2},{1,3},{2,0},{3,1},{4,6},{5,7},{6,4},{7,5},{8,10},{9,11},{10,... | collective-permute-start | bytes 589832 | tf_op jit(solution)/shard_map/ppermute | solution.py:25
  9.0 4.5 %collective-permute-done.arrived_ref = f32[32,1536]{1,0:T(8,128)S(1)} collective-permute-done((f32[32,1536]{1,0:T(8,128)S(1)}, f32[32,1536]{1,0:T(8,128)S(1)}, u32[]{:S(2)}, u32[]{:S(2)}) %collective-permute-start) | collective-permute-done | bytes 196640 | tf_op jit(solution)/shard_map/ppermute | solution.py:25
  13.5 4.5 %collective-permute-start.1 = (f32[64,256]{1,0:T(8,128)S(1)}, f32[64,256]{1,0:T(8,128)S(1)}, u32[]{:S(2)}, u32[]{:S(2)}) collective-permute-start(f32[64,256]{1,0:T(8,128)S(1)} %get-tuple-element.28.held_ref), channel_id=1, source_target_pairs={{0,4},{2,6},{4,0},{6,2},{8,12},{10,14},{12,8},{14,10},{16,20},{18,... | collective-permute-start | bytes 196616 | tf_op jit(solution)/shard_map/ppermute | solution.py:439
  18.0 2.6 %collective-permute-done.1.refs_0_ = f32[64,256]{1,0:T(8,128)S(1)} collective-permute-done((f32[64,256]{1,0:T(8,128)S(1)}, f32[64,256]{1,0:T(8,128)S(1)}, u32[]{:S(2)}, u32[]{:S(2)}) %collective-permute-start.1) | collective-permute-done | bytes 65568 | tf_op jit(solution)/shard_map/ppermute | solution.py:439
  20.7 1.2 %collective-permute-done.2.refs_0_ = f32[64,256]{1,0:T(8,128)S(1)} collective-permute-done((f32[64,256]{1,0:T(8,128)S(1)}, f32[64,256]{1,0:T(8,128)S(1)}, u32[]{:S(2)}, u32[]{:S(2)}) %collective-permute-start.2) | collective-permute-done | bytes 65568 | tf_op jit(solution)/shard_map/ppermute | solution.py:439
  22.7 3.8 %collective-permute-done.3.refs_0_.refs_1_ = f32[72,256]{1,0:T(8,128)S(1)} collective-permute-done((f32[72,256]{1,0:T(8,128)S(1)}, f32[72,256]{1,0:T(8,128)S(1)}, u32[]{:S(2)}, u32[]{:S(2)}) %collective-permute-start.3) | collective-permute-done | bytes 73760 | tf_op jit(solution)/shard_map/ppermute | solution.py:25
  27.1 3.8 %collective-permute-done.4.refs_3_.refs_1_ = f32[72,256]{1,0:T(8,128)S(1)} collective-permute-done((f32[72,256]{1,0:T(8,128)S(1)}, f32[72,256]{1,0:T(8,128)S(1)}, u32[]{:S(2)}, u32[]{:S(2)}) %collective-permute-start.4) | collective-permute-done | bytes 73760 | tf_op jit(solution)/shard_map/ppermute | solution.py:25
  33.5 1.7 %collective-permute-start.15 = (f32[32,1536]{1,0:T(8,128)S(1)}, f32[32,1536]{1,0:T(8,128)S(1)}, u32[]{:S(2)}, u32[]{:S(2)}) collective-permute-start(f32[32,1536]{1,0:T(8,128)S(1)} %get-tuple-element.43), channel_id=1, source_target_pairs={{0,2},{1,3},{2,0},{3,1},{4,6},{5,7},{6,4},{7,5},{8,10},{9,11},{10,... | collective-permute-start | bytes 589832 | tf_op jit(solution)/shard_map/ppermute | solution.py:25
  35.5 1.7 %collective-permute-start.9 = (f32[32,1024]{1,0:T(8,128)S(1)}, f32[32,1024]{1,0:T(8,128)S(1)}, u32[]{:S(2)}, u32[]{:S(2)}) collective-permute-start(f32[32,1024]{1,0:T(8,128)S(1)} %get-tuple-element.39), channel_id=1, source_target_pairs={{0,2},{1,3},{2,0},{3,1},{4,6},{5,7},{6,4},{7,5},{8,10},{9,11},{10,... | collective-permute-start | bytes 393224 | tf_op jit(solution)/shard_map/ppermute | solution.py:25
  37.3 5.3 %collective-permute-done.15.b_ref = f32[32,1536]{1,0:T(8,128)S(1)} collective-permute-done((f32[32,1536]{1,0:T(8,128)S(1)}, f32[32,1536]{1,0:T(8,128)S(1)}, u32[]{:S(2)}, u32[]{:S(2)}) %collective-permute-start.15) | collective-permute-done | bytes 196640 | tf_op jit(solution)/shard_map/ppermute | solution.py:25
  42.5 3.1 %collective-permute-start.18 = (f32[32,1024]{1,0:T(8,128)S(1)}, f32[32,1024]{1,0:T(8,128)S(1)}, u32[]{:S(2)}, u32[]{:S(2)}) collective-permute-start(f32[32,1024]{1,0:T(8,128)S(1)} %get-tuple-element.44.a_ref), channel_id=1, source_target_pairs={{0,4},{1,5},{2,6},{3,7},{4,0},{5,1},{6,2},{7,3},{8,12},{9,13},{10,... | collective-permute-start | bytes 393224 | tf_op jit(solution)/shard_map/ppermute | solution.py:25
  45.6 1.9 %collective-permute-done.12.b_ref = f32[32,1536]{1,0:T(8,128)S(1)} collective-permute-done((f32[32,1536]{1,0:T(8,128)S(1)}, f32[32,1536]{1,0:T(8,128)S(1)}, u32[]{:S(2)}, u32[]{:S(2)}) %collective-permute-start.12) | collective-permute-done | bytes 196640 | tf_op jit(solution)/shard_map/ppermute | solution.py:25
  47.5 1.7 %collective-permute-start.16 = (f32[32,1536]{1,0:T(8,128)S(1)}, f32[32,1536]{1,0:T(8,128)S(1)}, u32[]{:S(2)}, u32[]{:S(2)}) collective-permute-start(f32[32,1536]{1,0:T(8,128)S(1)} %shard_map.98.a_ref), channel_id=1, source_target_pairs={{0,4},{1,5},{2,6},{3,7},{4,0},{5,1},{6,2},{7,3},{8,12},{9,13},{10,... | collective-permute-start | bytes 589832 | tf_op jit(solution)/shard_map/ppermute | solution.py:25
  49.3 1.0 %collective-permute-done.9.b_ref = f32[32,1024]{1,0:T(8,128)S(1)} collective-permute-done((f32[32,1024]{1,0:T(8,128)S(1)}, f32[32,1024]{1,0:T(8,128)S(1)}, u32[]{:S(2)}, u32[]{:S(2)}) %collective-permute-start.9) | collective-permute-done | bytes 131104 | tf_op jit(solution)/shard_map/ppermute | solution.py:25
  50.3 0.9 %collective-permute-start.13 = (f32[32,1536]{1,0:T(8,128)S(1)}, f32[32,1536]{1,0:T(8,128)S(1)}, u32[]{:S(2)}, u32[]{:S(2)}) collective-permute-start(f32[32,1536]{1,0:T(8,128)S(1)} %shard_map.96.a_ref), channel_id=1, source_target_pairs={{0,4},{1,5},{2,6},{3,7},{4,0},{5,1},{6,2},{7,3},{8,12},{9,13},{10,... | collective-permute-start | bytes 589832 | tf_op jit(solution)/shard_map/ppermute | solution.py:25
  51.2 8.8 %collective-permute-done.18.b_ref = f32[32,1024]{1,0:T(8,128)S(1)} collective-permute-done((f32[32,1024]{1,0:T(8,128)S(1)}, f32[32,1024]{1,0:T(8,128)S(1)}, u32[]{:S(2)}, u32[]{:S(2)}) %collective-permute-start.18) | collective-permute-done | bytes 131104 | tf_op jit(solution)/shard_map/ppermute | solution.py:25
  60.0 4.7 %collective-permute-done.16.b_ref = f32[32,1536]{1,0:T(8,128)S(1)} collective-permute-done((f32[32,1536]{1,0:T(8,128)S(1)}, f32[32,1536]{1,0:T(8,128)S(1)}, u32[]{:S(2)}, u32[]{:S(2)}) %collective-permute-start.16) | collective-permute-done | bytes 196640 | tf_op jit(solution)/shard_map/ppermute | solution.py:25
  64.7 1.3 %collective-permute-start.19 = (f32[32,1024]{1,0:T(8,128)S(1)}, f32[32,1024]{1,0:T(8,128)S(1)}, u32[]{:S(2)}, u32[]{:S(2)}) collective-permute-start(f32[32,1024]{1,0:T(8,128)S(1)} %shard_map.100.piece_ref), channel_id=1, source_target_pairs={{0,2},{1,3},{2,0},{3,1},{4,6},{5,7},{6,4},{7,5},{8,10},{9,11},{10,... | collective-permute-start | bytes 393224 | tf_op jit(solution)/shard_map/ppermute | solution.py:25
  66.0 2.1 %collective-permute-done.13.b_ref = f32[32,1536]{1,0:T(8,128)S(1)} collective-permute-done((f32[32,1536]{1,0:T(8,128)S(1)}, f32[32,1536]{1,0:T(8,128)S(1)}, u32[]{:S(2)}, u32[]{:S(2)}) %collective-permute-start.13) | collective-permute-done | bytes 196640 | tf_op jit(solution)/shard_map/ppermute | solution.py:25
  68.2 1.4 %collective-permute-done.10.b_ref = f32[32,1024]{1,0:T(8,128)S(1)} collective-permute-done((f32[32,1024]{1,0:T(8,128)S(1)}, f32[32,1024]{1,0:T(8,128)S(1)}, u32[]{:S(2)}, u32[]{:S(2)}) %collective-permute-start.10) | collective-permute-done | bytes 131104 | tf_op jit(solution)/shard_map/ppermute | solution.py:25
  70.3 2.1 %collective-permute-done.19.arrived_ref = f32[32,1024]{1,0:T(8,128)S(1)} collective-permute-done((f32[32,1024]{1,0:T(8,128)S(1)}, f32[32,1024]{1,0:T(8,128)S(1)}, u32[]{:S(2)}, u32[]{:S(2)}) %collective-permute-start.19) | collective-permute-done | bytes 131104 | tf_op jit(solution)/shard_map/ppermute | solution.py:25
  72.3 1.3 %shard_map.101.refs_0_ = f32[64,5120]{1,0:T(8,128)} custom-call(s32[1,2]{1,0:T(1,128)S(1)} %copy-done.1, f32[32,1024]{1,0:T(8,128)S(1)} %shard_map.100.piece_ref, f32[32,1024]{1,0:T(8,128)S(1)} %collective-permute-done.19.arrived_ref), custom_call_target="tpu_custom_call" | custom-call | tf_op jit(solution)/shard_map/pallas_call | solution.py:60
  73.6 2.9 %collective-permute-done.17.arrived_ref = f32[32,1536]{1,0:T(8,128)S(1)} collective-permute-done((f32[32,1536]{1,0:T(8,128)S(1)}, f32[32,1536]{1,0:T(8,128)S(1)}, u32[]{:S(2)}, u32[]{:S(2)}) %collective-permute-start.17) | collective-permute-done | bytes 196640 | tf_op jit(solution)/shard_map/ppermute | solution.py:25
  76.5 1.3 %shard_map.102.refs_0_ = f32[64,5120]{1,0:T(8,128)} custom-call(s32[1,2]{1,0:T(1,128)S(1)} %copy-done.1, f32[32,1536]{1,0:T(8,128)S(1)} %shard_map.99.piece_ref, f32[32,1536]{1,0:T(8,128)S(1)} %collective-permute-done.17.arrived_ref, f32[64,5120]{1,0:T(8,128)} %shard_map.101.refs_0_), custom_call_target="tpu_custom_call", output_to_operand_aliasing={{}: (3, {})} | custom-call | tf_op jit(solution)/shard_map/pallas_call | solution.py:60
  77.9 1.4 %collective-permute-done.14.arrived_ref = f32[32,1536]{1,0:T(8,128)S(1)} collective-permute-done((f32[32,1536]{1,0:T(8,128)S(1)}, f32[32,1536]{1,0:T(8,128)S(1)}, u32[]{:S(2)}, u32[]{:S(2)}) %collective-permute-start.14) | collective-permute-done | bytes 196640 | tf_op jit(solution)/shard_map/ppermute | solution.py:25
  79.3 1.3 %shard_map.103.refs_0_ = f32[64,5120]{1,0:T(8,128)} custom-call(s32[1,2]{1,0:T(1,128)S(1)} %copy-done.1, f32[32,1536]{1,0:T(8,128)S(1)} %shard_map.97.piece_ref, f32[32,1536]{1,0:T(8,128)S(1)} %collective-permute-done.14.arrived_ref, f32[64,5120]{1,0:T(8,128)} %shard_map.102.refs_0_), custom_call_target="tpu_custom_call", output_to_operand_aliasing={{}: (3, {})} | custom-call | tf_op jit(solution)/shard_map/pallas_call | solution.py:60
  80.7 1.3 %shard_map.104 = f32[64,5120]{1,0:T(8,128)} custom-call(s32[1,2]{1,0:T(1,128)S(1)} %copy-done.1, f32[32,1024]{1,0:T(8,128)S(1)} %shard_map.95.piece_ref, f32[32,1024]{1,0:T(8,128)S(1)} %collective-permute-done.11.arrived_ref, f32[64,5120]{1,0:T(8,128)} %shard_map.103.refs_0_), custom_call_target="tpu_custom_call", output_to_operand_aliasing={{}: (3, {})} | custom-call | tf_op jit(solution)/shard_map/pallas_call | solution.py:60
  82.0 0.9 %shard_map.92 = (f32[64,5120]{1,0:T(8,128)}, f32[2,5120]{1,0:T(2,128)}) custom-call(f32[64,2560]{1,0:T(8,128)S(1)} %get-tuple-element.31.refs_4_.matrix_ref, f32[2,5120]{1,0:T(2,128)S(1)} %copy-done, f32[64,2688]{1,0:T(8,128)S(1)} %get-tuple-element.32.kept_ref, f32[64,2688]{1,0:T(8,128)S(1)} %collective-permute-done.8.arrived_ref), custom_call_target="tpu_custom_call" | custom-call | tf_op jit(solution)/shard_map/pallas_call | solution.py:60
  83.0 0.9 %shard_map.93 = (f32[64,5120]{1,0:T(8,128)}, f32[2,5120]{1,0:T(2,128)}) custom-call(f32[64,2560]{1,0:T(8,128)S(1)} %get-tuple-element.24.refs_4_.matrix_ref, f32[2,5120]{1,0:T(2,128)S(1)} %copy-done, f32[64,2688]{1,0:T(8,128)S(1)} %get-tuple-element.29.kept_ref, ...), custom_call_target="tpu_custom_call", output_to_operand_aliasing={{0}: (4, {}), {1}: (5, {})} | custom-call | tf_op jit(solution)/shard_map/pallas_call | solution.py:60
  (36 shorter events, 5.2 us)
Async XLA Ops:
  0.6 21.3 %copy-start.3 = (f32[2,64]{1,0:T(2,128)S(1)}, f32[2,64]{1,0:T(2,128)}, u32[]{:S(2)}) copy-start(f32[2,64]{1,0:T(2,128)} %weights_ref.1) | copy-start | bytes 1540
  0.6 30.3 %copy-start.2 = (s32[256]{0:T(256)S(1)}, s32[256]{0:T(256)}, u32[]{:S(2)}) copy-start(s32[256]{0:T(256)} %param.7) | copy-start | bytes 3076
  2.9 28.0 %collective-permute-start.7 = (f32[64,2560]{1,0:T(8,128)S(1)}, f32[64,2560]{1,0:T(8,128)S(1)}, u32[]{:S(2)}, u32[]{:S(2)}) collective-permute-start(f32[64,2560]{1,0:T(8,128)S(1)} %get-tuple-element.31.refs_4_.matrix_ref), channel_id=1, source_target_pairs={{0,8},{8,0},{16,24},{24,16},{1,9},{9,1},{17,25},{25,17},{2,10},{10... | collective-permute-start | bytes 1966088 | tf_op jit(solution)/shard_map/ppermute | solution.py:25
  5.9 26.4 %collective-permute-start.5 = (f32[64,2560]{1,0:T(8,128)S(1)}, f32[64,2560]{1,0:T(8,128)S(1)}, u32[]{:S(2)}, u32[]{:S(2)}) collective-permute-start(f32[64,2560]{1,0:T(8,128)S(1)} %get-tuple-element.24.refs_4_.matrix_ref), channel_id=1, source_target_pairs={{0,16},{8,24},{16,0},{24,8},{1,17},{9,25},{17,1},{25,9},{2,18},{10... | collective-permute-start | bytes 1966088 | tf_op jit(solution)/shard_map/ppermute | solution.py:25
  7.4 6.1 %collective-permute-start = (f32[32,1536]{1,0:T(8,128)S(1)}, f32[32,1536]{1,0:T(8,128)S(1)}, u32[]{:S(2)}, u32[]{:S(2)}) collective-permute-start(f32[32,1536]{1,0:T(8,128)S(1)} %get-tuple-element.26), channel_id=1, source_target_pairs={{0,2},{1,3},{2,0},{3,1},{4,6},{5,7},{6,4},{7,5},{8,10},{9,11},{10,... | collective-permute-start | bytes 589832 | tf_op jit(solution)/shard_map/ppermute | solution.py:25
  13.5 7.1 %collective-permute-start.1 = (f32[64,256]{1,0:T(8,128)S(1)}, f32[64,256]{1,0:T(8,128)S(1)}, u32[]{:S(2)}, u32[]{:S(2)}) collective-permute-start(f32[64,256]{1,0:T(8,128)S(1)} %get-tuple-element.28.held_ref), channel_id=1, source_target_pairs={{0,4},{2,6},{4,0},{6,2},{8,12},{10,14},{12,8},{14,10},{16,20},{18,... | collective-permute-start | bytes 196616 | tf_op jit(solution)/shard_map/ppermute | solution.py:439
  20.6 1.3 %collective-permute-start.2 = (f32[64,256]{1,0:T(8,128)S(1)}, f32[64,256]{1,0:T(8,128)S(1)}, u32[]{:S(2)}, u32[]{:S(2)}) collective-permute-start(f32[64,256]{1,0:T(8,128)S(1)} %shard_map.87.held_ref), channel_id=1, source_target_pairs={{0,1},{1,0},{2,3},{3,2},{4,5},{5,4},{6,7},{7,6},{8,9},{9,8},{10,11... | collective-permute-start | bytes 196616 | tf_op jit(solution)/shard_map/ppermute | solution.py:439
  22.1 4.4 %collective-permute-start.3 = (f32[72,256]{1,0:T(8,128)S(1)}, f32[72,256]{1,0:T(8,128)S(1)}, u32[]{:S(2)}, u32[]{:S(2)}) collective-permute-start(f32[72,256]{1,0:T(8,128)S(1)} %shard_map.88.message_ref), channel_id=1, source_target_pairs={{0,8},{8,0},{16,24},{24,16},{1,9},{9,1},{17,25},{25,17},{2,10},{10... | collective-permute-start | bytes 221192 | tf_op jit(solution)/shard_map/ppermute | solution.py:25
  26.5 4.4 %collective-permute-start.4 = (f32[72,256]{1,0:T(8,128)S(1)}, f32[72,256]{1,0:T(8,128)S(1)}, u32[]{:S(2)}, u32[]{:S(2)}) collective-permute-start(f32[72,256]{1,0:T(8,128)S(1)} %shard_map.89.refs_0_.refs_2_), channel_id=1, source_target_pairs={{0,16},{8,24},{16,0},{24,8},{1,17},{9,25},{17,1},{25,9},{2,18},{10... | collective-permute-start | bytes 221192 | tf_op jit(solution)/shard_map/ppermute | solution.py:25
  31.7 50.3 %collective-permute-start.8 = (f32[64,2688]{1,0:T(8,128)S(1)}, f32[64,2688]{1,0:T(8,128)S(1)}, u32[]{:S(2)}, u32[]{:S(2)}) collective-permute-start(f32[64,2688]{1,0:T(8,128)S(1)} %get-tuple-element.33), channel_id=1, source_target_pairs={{0,16},{8,24},{16,0},{24,8},{1,17},{9,25},{17,1},{25,9},{2,18},{10... | collective-permute-start | bytes 2064392 | tf_op jit(solution)/shard_map/ppermute | solution.py:25
  33.1 49.9 %collective-permute-start.6 = (f32[64,2688]{1,0:T(8,128)S(1)}, f32[64,2688]{1,0:T(8,128)S(1)}, u32[]{:S(2)}, u32[]{:S(2)}) collective-permute-start(f32[64,2688]{1,0:T(8,128)S(1)} %get-tuple-element.30), channel_id=1, source_target_pairs={{0,8},{8,0},{16,24},{24,16},{1,9},{9,1},{17,25},{25,17},{2,10},{10... | collective-permute-start | bytes 2064392 | tf_op jit(solution)/shard_map/ppermute | solution.py:25
  33.5 9.0 %collective-permute-start.15 = (f32[32,1536]{1,0:T(8,128)S(1)}, f32[32,1536]{1,0:T(8,128)S(1)}, u32[]{:S(2)}, u32[]{:S(2)}) collective-permute-start(f32[32,1536]{1,0:T(8,128)S(1)} %get-tuple-element.43), channel_id=1, source_target_pairs={{0,2},{1,3},{2,0},{3,1},{4,6},{5,7},{6,4},{7,5},{8,10},{9,11},{10,... | collective-permute-start | bytes 589832 | tf_op jit(solution)/shard_map/ppermute | solution.py:25
  35.2 12.3 %collective-permute-start.12 = (f32[32,1536]{1,0:T(8,128)S(1)}, f32[32,1536]{1,0:T(8,128)S(1)}, u32[]{:S(2)}, u32[]{:S(2)}) collective-permute-start(f32[32,1536]{1,0:T(8,128)S(1)} %get-tuple-element.41), channel_id=1, source_target_pairs={{0,2},{1,3},{2,0},{3,1},{4,6},{5,7},{6,4},{7,5},{8,10},{9,11},{10,... | collective-permute-start | bytes 589832 | tf_op jit(solution)/shard_map/ppermute | solution.py:25
  35.5 14.8 %collective-permute-start.9 = (f32[32,1024]{1,0:T(8,128)S(1)}, f32[32,1024]{1,0:T(8,128)S(1)}, u32[]{:S(2)}, u32[]{:S(2)}) collective-permute-start(f32[32,1024]{1,0:T(8,128)S(1)} %get-tuple-element.39), channel_id=1, source_target_pairs={{0,2},{1,3},{2,0},{3,1},{4,6},{5,7},{6,4},{7,5},{8,10},{9,11},{10,... | collective-permute-start | bytes 393224 | tf_op jit(solution)/shard_map/ppermute | solution.py:25
  42.5 17.5 %collective-permute-start.18 = (f32[32,1024]{1,0:T(8,128)S(1)}, f32[32,1024]{1,0:T(8,128)S(1)}, u32[]{:S(2)}, u32[]{:S(2)}) collective-permute-start(f32[32,1024]{1,0:T(8,128)S(1)} %get-tuple-element.44.a_ref), channel_id=1, source_target_pairs={{0,4},{1,5},{2,6},{3,7},{4,0},{5,1},{6,2},{7,3},{8,12},{9,13},{10,... | collective-permute-start | bytes 393224 | tf_op jit(solution)/shard_map/ppermute | solution.py:25
  47.5 17.2 %collective-permute-start.16 = (f32[32,1536]{1,0:T(8,128)S(1)}, f32[32,1536]{1,0:T(8,128)S(1)}, u32[]{:S(2)}, u32[]{:S(2)}) collective-permute-start(f32[32,1536]{1,0:T(8,128)S(1)} %shard_map.98.a_ref), channel_id=1, source_target_pairs={{0,4},{1,5},{2,6},{3,7},{4,0},{5,1},{6,2},{7,3},{8,12},{9,13},{10,... | collective-permute-start | bytes 589832 | tf_op jit(solution)/shard_map/ppermute | solution.py:25
  49.3 23.1 %copy-start.1 = (s32[1,2]{1,0:T(1,128)S(1)}, s32[1,2]{1,0:T(1,128)}, u32[]{:S(2)}) copy-start(s32[1,2]{1,0:T(1,128)} %points_ref.7) | copy-start | bytes 28
  50.3 17.8 %collective-permute-start.13 = (f32[32,1536]{1,0:T(8,128)S(1)}, f32[32,1536]{1,0:T(8,128)S(1)}, u32[]{:S(2)}, u32[]{:S(2)}) collective-permute-start(f32[32,1536]{1,0:T(8,128)S(1)} %shard_map.96.a_ref), channel_id=1, source_target_pairs={{0,4},{1,5},{2,6},{3,7},{4,0},{5,1},{6,2},{7,3},{8,12},{9,13},{10,... | collective-permute-start | bytes 589832 | tf_op jit(solution)/shard_map/ppermute | solution.py:25
  60.0 9.6 %collective-permute-start.10 = (f32[32,1024]{1,0:T(8,128)S(1)}, f32[32,1024]{1,0:T(8,128)S(1)}, u32[]{:S(2)}, u32[]{:S(2)}) collective-permute-start(f32[32,1024]{1,0:T(8,128)S(1)} %shard_map.94.a_ref), channel_id=1, source_target_pairs={{0,4},{1,5},{2,6},{3,7},{4,0},{5,1},{6,2},{7,3},{8,12},{9,13},{10,... | collective-permute-start | bytes 393224 | tf_op jit(solution)/shard_map/ppermute | solution.py:25
  64.7 7.7 %collective-permute-start.19 = (f32[32,1024]{1,0:T(8,128)S(1)}, f32[32,1024]{1,0:T(8,128)S(1)}, u32[]{:S(2)}, u32[]{:S(2)}) collective-permute-start(f32[32,1024]{1,0:T(8,128)S(1)} %shard_map.100.piece_ref), channel_id=1, source_target_pairs={{0,2},{1,3},{2,0},{3,1},{4,6},{5,7},{6,4},{7,5},{8,10},{9,11},{10,... | collective-permute-start | bytes 393224 | tf_op jit(solution)/shard_map/ppermute | solution.py:25
  68.1 8.4 %collective-permute-start.17 = (f32[32,1536]{1,0:T(8,128)S(1)}, f32[32,1536]{1,0:T(8,128)S(1)}, u32[]{:S(2)}, u32[]{:S(2)}) collective-permute-start(f32[32,1536]{1,0:T(8,128)S(1)} %shard_map.99.piece_ref), channel_id=1, source_target_pairs={{0,2},{1,3},{2,0},{3,1},{4,6},{5,7},{6,4},{7,5},{8,10},{9,11},{10,... | collective-permute-start | bytes 589832 | tf_op jit(solution)/shard_map/ppermute | solution.py:25
  69.5 9.8 %collective-permute-start.14 = (f32[32,1536]{1,0:T(8,128)S(1)}, f32[32,1536]{1,0:T(8,128)S(1)}, u32[]{:S(2)}, u32[]{:S(2)}) collective-permute-start(f32[32,1536]{1,0:T(8,128)S(1)} %shard_map.97.piece_ref), channel_id=1, source_target_pairs={{0,2},{1,3},{2,0},{3,1},{4,6},{5,7},{6,4},{7,5},{8,10},{9,11},{10,... | collective-permute-start | bytes 589832 | tf_op jit(solution)/shard_map/ppermute | solution.py:25
  72.3 8.4 %collective-permute-start.11 = (f32[32,1024]{1,0:T(8,128)S(1)}, f32[32,1024]{1,0:T(8,128)S(1)}, u32[]{:S(2)}, u32[]{:S(2)}) collective-permute-start(f32[32,1024]{1,0:T(8,128)S(1)} %shard_map.95.piece_ref), channel_id=1, source_target_pairs={{0,2},{1,3},{2,0},{3,1},{4,6},{5,7},{6,4},{7,5},{8,10},{9,11},{10,... | collective-permute-start | bytes 393224 | tf_op jit(solution)/shard_map/ppermute | solution.py:25
  80.7 1.4 %copy-start = (f32[2,5120]{1,0:T(2,128)S(1)}, f32[2,5120]{1,0:T(2,128)}, u32[]{:S(2)}) copy-start(f32[2,5120]{1,0:T(2,128)} %checksum_ref.3) | copy-start | bytes 122884

commit v2 on v1

--- a/solution.py
+++ b/solution.py
@@ -6,7 +6,7 @@
 from jax.sharding import PartitionSpec as P
 
 
-CUTS = (0, 8, 20, 32, 40)
+STAGES = ((0, 8, 20, 32, 40), (0, 8, 20, 32, 40), (0, 20, 32, 40))
 LANES = 128
 GRANT = 8 << 20
 ROOM = 67_043_328
@@ -186,20 +186,40 @@
     return call(kernel, [a.shape], [VMEM, VMEM], [a, b])[0]
 
 
-def add_and_unpack(kept, arrived, panel, groups):
+def add_and_cut(kept, arrived, cuts, panel, groups):
     height, cols = kept.shape
-    rows, width = panel.shape
-
-    def kernel(kept_ref, arrived_ref, held_ref, out_ref, panel_ref):
-        out_ref[...] = kept_ref[...] + arrived_ref[:, :cols]
-        came = lax.axis_index("col") // groups & 1 == 1
-        for k in range(rows // height):
-            lines = slice(k * height, (k + 1) * height)
-            there = slice(cols + k * width, cols + (k + 1) * width)
-            panel_ref[lines, :] = jnp.where(came, arrived_ref[:, there], held_ref[lines, :])
-
-    shapes = [kept.shape, panel.shape]
-    return call(kernel, shapes, [VMEM] * 3, [kept, arrived, panel])
+    count = len(cuts) - 1
+    held = [] if panel is None else [panel]
+
+    def kernel(kept_ref, arrived_ref, *refs):
+        out_refs = refs[len(held) :]
+        for low, high, out_ref in zip(cuts, cuts[1:], out_refs):
+            out_ref[...] = kept_ref[:, low:high] + arrived_ref[:, low:high]
+        if held:
+            rows, width = refs[0].shape
+            came = lax.axis_index("col") // groups & 1 == 1
+            for k in range(rows // height):
+                lines = slice(k * height, (k + 1) * height)
+                there = slice(cols + k * width, cols + (k + 1) * width)
+                out_refs[count][lines, :] = jnp.where(came, arrived_ref[:, there], refs[0][lines, :])
+
+    shapes = [(height, high - low) for low, high in zip(cuts, cuts[1:])]
+    shapes += [panel.shape for panel in held]
+    return call(kernel, shapes, [VMEM] * (2 + len(held)), [kept, arrived, *held])
+
+
+def add_and_join(pairs):
+    height = pairs[0][0].shape[0]
+    widths = [a.shape[1] for a, _ in pairs]
+
+    def kernel(*refs):
+        low = 0
+        for k, width in enumerate(widths):
+            refs[-1][:, low : low + width] = refs[2 * k][...] + refs[2 * k + 1][...]
+            low += width
+
+    operands = [value for pair in pairs for value in pair]
+    return call(kernel, [(height, sum(widths))], [VMEM] * len(operands), operands)[0]
 
 
 def split(value, terms):
@@ -399,9 +419,12 @@
     plans = plans_of(n_row)
 
     position = col_index // groups
-    cuts = [cut * (cols // LANES) // CUTS[-1] * LANES for cut in CUTS]
+    stage_cuts = [
+        [cut * (cols // LANES) // ends[-1] * LANES for cut in ends] for ends in STAGES
+    ]
     members = n_col // groups
     carry = len(bits_of(members)) == 2 and groups == 2
+    cuts = stage_cuts[0]
     sides, lower, parts = prepare(matrix, coefficients, groups, cuts, width, carry)
 
     gathered = []
@@ -416,13 +439,12 @@
                 blocks += [arrived[i * rows : (i + 1) * rows] for i in range(len(blocks))]
         gathered.append(blocks)
 
-    codes = []
     stages = panel_stages(n_col)
+    firsts = []
     if carry:
         arrived = swap(parts[0][0], "col", groups)
-        piece, lower = add_and_unpack(parts[0][1], arrived, lower, groups)
-        arrived = swap(piece, "col", 2 * groups)
-        codes.append(add(piece, arrived))
+        inside = [cut for cut in stage_cuts[1] if cut <= cuts[1]]
+        *firsts, lower = add_and_cut(parts[0][1], arrived, inside, lower, groups)
         stages = [[2], [0]]
     for number, bits in enumerate(stages):
         masks = span(bits)[1:]
@@ -474,12 +496,26 @@
             number, sides[number], checksum, width, part[0], arrived, results
         )
 
-    for chunk in range(len(codes), len(parts)):
-        codes.append(reduce_code(*parts[chunk], groups, position, members))
+    finals = []
+    if carry:
+        for k in range(1, len(parts)):
+            low, high = cuts[k], cuts[k + 1]
+            arrived = swap(parts[k][0], "col", groups)
+            inside = [cut - low for cut in stage_cuts[1] if low <= cut <= high]
+            firsts += add_and_cut(parts[k][1], arrived, inside, None, groups)
+        pairs = [(a, swap(a, "col", 2 * groups)) for a in firsts]
+        cuts = stage_cuts[2]
+        for low, high in zip(cuts, cuts[1:]):
+            mine = [pairs[j] for j, cut in enumerate(stage_cuts[1][:-1]) if low <= cut < high]
+            piece = add_and_join(mine)
+            finals.append((piece, swap(piece, "col", groups)))
+    else:
+        for part in parts:
+            piece = reduce_code(*part, groups, position, members)
+            finals.append(gather_code(piece, groups, position, members))
     parity = ()
-    for chunk, piece in enumerate(codes):
-        piece, arrived = gather_code(piece, groups, position, members)
-        parity = store_code(checkpoints, cuts[chunk], piece, arrived, (rows, cols), parity)
+    for k, (piece, arrived) in enumerate(finals):
+        parity = store_code(checkpoints, cuts[k], piece, arrived, (rows, cols), parity)
     return (*results, *parity)
 
 

time: 84.1 us -> 76.4 us (0.908)
  waiting for transfers between devices: 47.6 us -> 37.4 us
  starting transfers between devices: 24.3 us -> 27.8 us
  Pallas kernels: 10.5 us -> 9.38 us
    ppermute x18 -> x17, waiting for transfers between devices: 43.8 us -> 33.7 us  [swap(): lax.ppermute(value, axis, [(i, i ^ mask) for i in range(lax.axis_size(axi...]
    ppermute x18 -> x17, starting transfers between devices: 19.7 us -> 23.3 us  [swap(): lax.ppermute(value, axis, [(i, i ^ mask) for i in range(lax.axis_size(axi...]
    pallas_call x20 -> x18, Pallas kernels: 10.5 us -> 9.38 us  [call(): pl.pallas_call(kernel, out_shape=outs, in_specs=in_specs, out_specs=place...]
  transfers between devices with their start and end apart: 20 -> 19, of which waited for: 15 -> 10; matrix products, arithmetic and copies ran while one was open for 0% -> 0% of each run, Pallas kernels for 10% -> 9%
where the time goes in v2:
time: 76.4 us; the launch traced here: 76.2 us
  waiting for transfers between devices  37.4 us (49%)
  starting transfers between devices  27.8 us (36%)
  Pallas kernels  9.38 us (12%)
  between operations  1.49 us (2%)
    ppermute x17, waiting for transfers between devices, swap(): lax.ppermute(value, axis, [(i, i ^ mask) for i in range(lax.axis_size(axi...  33.7 us
    ppermute x17, starting transfers between devices, swap(): lax.ppermute(value, axis, [(i, i ^ mask) for i in range(lax.axis_size(axi...  23.3 us
    pallas_call x18, Pallas kernels, call(): pl.pallas_call(kernel, out_shape=outs, in_specs=in_specs, out_specs=place...  9.38 us
    ppermute x2, starting transfers between devices, per_device(): came.append(lax.ppermute(lower, 'col', route))  4.57 us
    ppermute x2, waiting for transfers between devices, per_device(): came.append(lax.ppermute(lower, 'col', route))  3.79 us
  transfers between devices with their start and end apart: 19, of which 10 were waited for; matrix products, arithmetic and copies ran while one was open for 0% of the time, Pallas kernels for 9%

profile of v2, /device:TPU:0, one launch (start us, length us, event | category | flops | bytes accessed | tf_op | source)
XLA Modules:
  0.0 76.2 jit_solution(15456559113697640116)
XLA Ops:
  1.3 1.6 %shard_map.85 = (f32[64,2560]{1,0:T(8,128)S(1)}, f32[64,2560]{1,0:T(8,128)S(1)}, f32[64,256]{1,0:T(8,128)S(1)}, f32[32,1536]{1,0:T(8,128)S(1)}, f32[32,1024]{1,0...) custom-call(f32[64,5120]{1,0:T(8,128)} %matrix_ref.1, ...), custom_call_target="tpu_custom_call" | custom-call | tf_op jit(solution)/shard_map/pallas_call | solution.py:60
  2.9 3.0 %collective-permute-start.7 = (f32[64,2560]{1,0:T(8,128)S(1)}, f32[64,2560]{1,0:T(8,128)S(1)}, u32[]{:S(2)}, u32[]{:S(2)}) collective-permute-start(f32[64,2560]{1,0:T(8,128)S(1)} %get-tuple-element.31.refs_4_.matrix_ref), channel_id=1, source_target_pairs={{0,8},{8,0},{16,24},{24,16},{1,9},{9,1},{17,25},{25,17},{2,10},{10... | collective-permute-start | bytes 1966088 | tf_op jit(solution)/shard_map/ppermute | solution.py:25
  5.9 1.5 %collective-permute-start.5 = (f32[64,2560]{1,0:T(8,128)S(1)}, f32[64,2560]{1,0:T(8,128)S(1)}, u32[]{:S(2)}, u32[]{:S(2)}) collective-permute-start(f32[64,2560]{1,0:T(8,128)S(1)} %get-tuple-element.24.refs_4_.matrix_ref), channel_id=1, source_target_pairs={{0,16},{8,24},{16,0},{24,8},{1,17},{9,25},{17,1},{25,9},{2,18},{10... | collective-permute-start | bytes 1966088 | tf_op jit(solution)/shard_map/ppermute | solution.py:25
  7.4 1.6 %collective-permute-start = (f32[32,1536]{1,0:T(8,128)S(1)}, f32[32,1536]{1,0:T(8,128)S(1)}, u32[]{:S(2)}, u32[]{:S(2)}) collective-permute-start(f32[32,1536]{1,0:T(8,128)S(1)} %get-tuple-element.26), channel_id=1, source_target_pairs={{0,2},{1,3},{2,0},{3,1},{4,6},{5,7},{6,4},{7,5},{8,10},{9,11},{10,... | collective-permute-start | bytes 589832 | tf_op jit(solution)/shard_map/ppermute | solution.py:25
  9.0 4.5 %collective-permute-done.arrived_ref = f32[32,1536]{1,0:T(8,128)S(1)} collective-permute-done((f32[32,1536]{1,0:T(8,128)S(1)}, f32[32,1536]{1,0:T(8,128)S(1)}, u32[]{:S(2)}, u32[]{:S(2)}) %collective-permute-start) | collective-permute-done | bytes 196640 | tf_op jit(solution)/shard_map/ppermute | solution.py:25
  13.5 4.5 %collective-permute-start.1 = (f32[64,256]{1,0:T(8,128)S(1)}, f32[64,256]{1,0:T(8,128)S(1)}, u32[]{:S(2)}, u32[]{:S(2)}) collective-permute-start(f32[64,256]{1,0:T(8,128)S(1)} %get-tuple-element.28.held_ref), channel_id=1, source_target_pairs={{0,4},{2,6},{4,0},{6,2},{8,12},{10,14},{12,8},{14,10},{16,20},{18,... | collective-permute-start | bytes 196616 | tf_op jit(solution)/shard_map/ppermute | solution.py:461
  18.0 2.6 %collective-permute-done.1.refs_0_ = f32[64,256]{1,0:T(8,128)S(1)} collective-permute-done((f32[64,256]{1,0:T(8,128)S(1)}, f32[64,256]{1,0:T(8,128)S(1)}, u32[]{:S(2)}, u32[]{:S(2)}) %collective-permute-start.1) | collective-permute-done | bytes 65568 | tf_op jit(solution)/shard_map/ppermute | solution.py:461
  20.7 1.2 %collective-permute-done.2.refs_0_ = f32[64,256]{1,0:T(8,128)S(1)} collective-permute-done((f32[64,256]{1,0:T(8,128)S(1)}, f32[64,256]{1,0:T(8,128)S(1)}, u32[]{:S(2)}, u32[]{:S(2)}) %collective-permute-start.2) | collective-permute-done | bytes 65568 | tf_op jit(solution)/shard_map/ppermute | solution.py:461
  21.9 0.2 shard_map.88.message_ref
  22.1 0.5 collective-permute-start.3
  22.7 3.8 %collective-permute-done.3.refs_0_.refs_1_ = f32[72,256]{1,0:T(8,128)S(1)} collective-permute-done((f32[72,256]{1,0:T(8,128)S(1)}, f32[72,256]{1,0:T(8,128)S(1)}, u32[]{:S(2)}, u32[]{:S(2)}) %collective-permute-start.3) | collective-permute-done | bytes 73760 | tf_op jit(solution)/shard_map/ppermute | solution.py:25
  26.5 0.6 collective-permute-start.4
  27.1 1.6 %collective-permute-start.16 = (f32[32,1536]{1,0:T(8,128)S(1)}, f32[32,1536]{1,0:T(8,128)S(1)}, u32[]{:S(2)}, u32[]{:S(2)}) collective-permute-start(f32[32,1536]{1,0:T(8,128)S(1)} %get-tuple-element.44), channel_id=1, source_target_pairs={{0,2},{1,3},{2,0},{3,1},{4,6},{5,7},{6,4},{7,5},{8,10},{9,11},{10,... | collective-permute-start | bytes 589832 | tf_op jit(solution)/shard_map/ppermute | solution.py:25
  28.6 2.3 %collective-permute-done.4.refs_3_.refs_1_ = f32[72,256]{1,0:T(8,128)S(1)} collective-permute-done((f32[72,256]{1,0:T(8,128)S(1)}, f32[72,256]{1,0:T(8,128)S(1)}, u32[]{:S(2)}, u32[]{:S(2)}) %collective-permute-start.4) | collective-permute-done | bytes 73760 | tf_op jit(solution)/shard_map/ppermute | solution.py:25
  30.9 0.8 %shard_map.91 = (f32[64,2688]{1,0:T(8,128)S(1)}, f32[64,2688]{1,0:T(8,128)S(1)}) custom-call(s32[1,256]{1,0:T(1,128)S(1)} %bitcast.1, f32[72,256]{1,0:T(8,128)S(1)} %shard_map.89.refs_0_.refs_2_, f32[72,256]{1,0:T(8,128)S(1)} %collective-permute-done.4.refs_3_.refs_1_, f32[72,256]{1,0:T(8,128)S(1)} %shard_map.89.refs_0_.refs_2_, ...), custom_call_target="tpu_custom_call" | custom-call | flops 89128960 | tf_op jit(solution)/shard_map/pallas_call | solution.py:60
  31.7 0.6 collective-permute-start.8
  32.3 0.8 %shard_map.90 = (f32[64,2688]{1,0:T(8,128)S(1)}, f32[64,2688]{1,0:T(8,128)S(1)}) custom-call(s32[1,256]{1,0:T(1,128)S(1)} %bitcast.2, f32[72,256]{1,0:T(8,128)S(1)} %shard_map.89.refs_0_.refs_2_, f32[72,256]{1,0:T(8,128)S(1)} %collective-permute-done.3.refs_0_.refs_1_, f32[72,256]{1,0:T(8,128)S(1)} %shard_map.89.refs_0_.refs_2_, ...), custom_call_target="tpu_custom_call" | custom-call | flops 89128960 | tf_op jit(solution)/shard_map/pallas_call | solution.py:60
  33.1 0.4 collective-permute-start.6
  33.5 1.7 %collective-permute-start.12 = (f32[32,1536]{1,0:T(8,128)S(1)}, f32[32,1536]{1,0:T(8,128)S(1)}, u32[]{:S(2)}, u32[]{:S(2)}) collective-permute-start(f32[32,1536]{1,0:T(8,128)S(1)} %get-tuple-element.41), channel_id=1, source_target_pairs={{0,2},{1,3},{2,0},{3,1},{4,6},{5,7},{6,4},{7,5},{8,10},{9,11},{10,... | collective-permute-start | bytes 589832 | tf_op jit(solution)/shard_map/ppermute | solution.py:25
  35.3 3.3 %collective-permute-start.17 = (f32[32,1536]{1,0:T(8,128)S(1)}, f32[32,1536]{1,0:T(8,128)S(1)}, u32[]{:S(2)}, u32[]{:S(2)}) collective-permute-start(f32[32,1536]{1,0:T(8,128)S(1)} %shard_map.98.refs_2_), channel_id=1, source_target_pairs={{0,4},{1,5},{2,6},{3,7},{4,0},{5,1},{6,2},{7,3},{8,12},{9,13},{10,... | collective-permute-start | bytes 589832 | tf_op jit(solution)/shard_map/ppermute | solution.py:25
  38.6 5.2 %collective-permute-done.12.arrived_ref = f32[32,1536]{1,0:T(8,128)S(1)} collective-permute-done((f32[32,1536]{1,0:T(8,128)S(1)}, f32[32,1536]{1,0:T(8,128)S(1)}, u32[]{:S(2)}, u32[]{:S(2)}) %collective-permute-start.12) | collective-permute-done | bytes 196640 | tf_op jit(solution)/shard_map/ppermute | solution.py:25
  43.8 7.5 %collective-permute-done.15.refs_1_ = f32[32,1024]{1,0:T(8,128)S(1)} collective-permute-done((f32[32,1024]{1,0:T(8,128)S(1)}, f32[32,1024]{1,0:T(8,128)S(1)}, u32[]{:S(2)}, u32[]{:S(2)}) %collective-permute-start.15) | collective-permute-done | bytes 131104 | tf_op jit(solution)/shard_map/ppermute | solution.py:25
  51.3 4.9 %collective-permute-start.18 = (f32[32,2560]{1,0:T(8,128)S(1)}, f32[32,2560]{1,0:T(8,128)S(1)}, u32[]{:S(2)}, u32[]{:S(2)}) collective-permute-start(f32[32,2560]{1,0:T(8,128)S(1)} %shard_map.99.piece_ref), channel_id=1, source_target_pairs={{0,2},{1,3},{2,0},{3,1},{4,6},{5,7},{6,4},{7,5},{8,10},{9,11},{10,... | collective-permute-start | bytes 983048 | tf_op jit(solution)/shard_map/ppermute | solution.py:25
  56.4 5.5 %collective-permute-done.13.refs_1_ = f32[32,1536]{1,0:T(8,128)S(1)} collective-permute-done((f32[32,1536]{1,0:T(8,128)S(1)}, f32[32,1536]{1,0:T(8,128)S(1)}, u32[]{:S(2)}, u32[]{:S(2)}) %collective-permute-start.13) | collective-permute-done | bytes 196640 | tf_op jit(solution)/shard_map/ppermute | solution.py:25
  61.8 0.2 collective-permute-start.14
  62.0 4.8 %collective-permute-done.10.refs_1_ = f32[32,1024]{1,0:T(8,128)S(1)} collective-permute-done((f32[32,1024]{1,0:T(8,128)S(1)}, f32[32,1024]{1,0:T(8,128)S(1)}, u32[]{:S(2)}, u32[]{:S(2)}) %collective-permute-start.10) | collective-permute-done | bytes 131104 | tf_op jit(solution)/shard_map/ppermute | solution.py:25
  66.9 3.2 %collective-permute-start.11 = (f32[32,1024]{1,0:T(8,128)S(1)}, f32[32,1024]{1,0:T(8,128)S(1)}, u32[]{:S(2)}, u32[]{:S(2)}) collective-permute-start(f32[32,1024]{1,0:T(8,128)S(1)} %shard_map.95.piece_ref), channel_id=1, source_target_pairs={{0,2},{1,3},{2,0},{3,1},{4,6},{5,7},{6,4},{7,5},{8,10},{9,11},{10,... | collective-permute-start | bytes 393224 | tf_op jit(solution)/shard_map/ppermute | solution.py:25
  70.1 1.5 %shard_map.100.refs_0_ = f32[64,5120]{1,0:T(8,128)} custom-call(s32[1,2]{1,0:T(1,128)S(1)} %copy-done.1, f32[32,2560]{1,0:T(8,128)S(1)} %shard_map.99.piece_ref, f32[32,2560]{1,0:T(8,128)S(1)} %collective-permute-done.18.arrived_ref), custom_call_target="tpu_custom_call" | custom-call | tf_op jit(solution)/shard_map/pallas_call | solution.py:60
  71.5 1.3 %shard_map.101.refs_0_ = f32[64,5120]{1,0:T(8,128)} custom-call(s32[1,2]{1,0:T(1,128)S(1)} %copy-done.1, f32[32,1536]{1,0:T(8,128)S(1)} %shard_map.97.piece_ref, f32[32,1536]{1,0:T(8,128)S(1)} %collective-permute-done.14.arrived_ref, f32[64,5120]{1,0:T(8,128)} %shard_map.100.refs_0_), custom_call_target="tpu_custom_call", output_to_operand_aliasing={{}: (3, {})} | custom-call | tf_op jit(solution)/shard_map/pallas_call | solution.py:60
  73.0 1.3 %shard_map.102 = f32[64,5120]{1,0:T(8,128)} custom-call(s32[1,2]{1,0:T(1,128)S(1)} %copy-done.1, f32[32,1024]{1,0:T(8,128)S(1)} %shard_map.95.piece_ref, f32[32,1024]{1,0:T(8,128)S(1)} %collective-permute-done.11.arrived_ref, f32[64,5120]{1,0:T(8,128)} %shard_map.101.refs_0_), custom_call_target="tpu_custom_call", output_to_operand_aliasing={{}: (3, {})} | custom-call | tf_op jit(solution)/shard_map/pallas_call | solution.py:60
  74.3 0.9 %shard_map.92 = (f32[64,5120]{1,0:T(8,128)}, f32[2,5120]{1,0:T(2,128)}) custom-call(f32[64,2560]{1,0:T(8,128)S(1)} %get-tuple-element.31.refs_4_.matrix_ref, f32[2,5120]{1,0:T(2,128)S(1)} %copy-done, f32[64,2688]{1,0:T(8,128)S(1)} %get-tuple-element.32.kept_ref, f32[64,2688]{1,0:T(8,128)S(1)} %collective-permute-done.8.arrived_ref), custom_call_target="tpu_custom_call" | custom-call | tf_op jit(solution)/shard_map/pallas_call | solution.py:60
  75.3 0.9 %shard_map.93 = (f32[64,5120]{1,0:T(8,128)}, f32[2,5120]{1,0:T(2,128)}) custom-call(f32[64,2560]{1,0:T(8,128)S(1)} %get-tuple-element.24.refs_4_.matrix_ref, f32[2,5120]{1,0:T(2,128)S(1)} %copy-done, f32[64,2688]{1,0:T(8,128)S(1)} %get-tuple-element.29.kept_ref, ...), custom_call_target="tpu_custom_call", output_to_operand_aliasing={{0}: (4, {}), {1}: (5, {})} | custom-call | tf_op jit(solution)/shard_map/pallas_call | solution.py:60
  (32 shorter events, 0.6 us)
Async XLA Ops:
  0.6 21.3 %copy-start.3 = (f32[2,64]{1,0:T(2,128)S(1)}, f32[2,64]{1,0:T(2,128)}, u32[]{:S(2)}) copy-start(f32[2,64]{1,0:T(2,128)} %weights_ref.1) | copy-start | bytes 1540
  0.6 30.3 %copy-start.2 = (s32[256]{0:T(256)S(1)}, s32[256]{0:T(256)}, u32[]{:S(2)}) copy-start(s32[256]{0:T(256)} %param.7) | copy-start | bytes 3076
  2.9 28.0 %collective-permute-start.7 = (f32[64,2560]{1,0:T(8,128)S(1)}, f32[64,2560]{1,0:T(8,128)S(1)}, u32[]{:S(2)}, u32[]{:S(2)}) collective-permute-start(f32[64,2560]{1,0:T(8,128)S(1)} %get-tuple-element.31.refs_4_.matrix_ref), channel_id=1, source_target_pairs={{0,8},{8,0},{16,24},{24,16},{1,9},{9,1},{17,25},{25,17},{2,10},{10... | collective-permute-start | bytes 1966088 | tf_op jit(solution)/shard_map/ppermute | solution.py:25
  5.9 26.4 %collective-permute-start.5 = (f32[64,2560]{1,0:T(8,128)S(1)}, f32[64,2560]{1,0:T(8,128)S(1)}, u32[]{:S(2)}, u32[]{:S(2)}) collective-permute-start(f32[64,2560]{1,0:T(8,128)S(1)} %get-tuple-element.24.refs_4_.matrix_ref), channel_id=1, source_target_pairs={{0,16},{8,24},{16,0},{24,8},{1,17},{9,25},{17,1},{25,9},{2,18},{10... | collective-permute-start | bytes 1966088 | tf_op jit(solution)/shard_map/ppermute | solution.py:25
  7.4 6.1 %collective-permute-start = (f32[32,1536]{1,0:T(8,128)S(1)}, f32[32,1536]{1,0:T(8,128)S(1)}, u32[]{:S(2)}, u32[]{:S(2)}) collective-permute-start(f32[32,1536]{1,0:T(8,128)S(1)} %get-tuple-element.26), channel_id=1, source_target_pairs={{0,2},{1,3},{2,0},{3,1},{4,6},{5,7},{6,4},{7,5},{8,10},{9,11},{10,... | collective-permute-start | bytes 589832 | tf_op jit(solution)/shard_map/ppermute | solution.py:25
  13.5 7.1 %collective-permute-start.1 = (f32[64,256]{1,0:T(8,128)S(1)}, f32[64,256]{1,0:T(8,128)S(1)}, u32[]{:S(2)}, u32[]{:S(2)}) collective-permute-start(f32[64,256]{1,0:T(8,128)S(1)} %get-tuple-element.28.held_ref), channel_id=1, source_target_pairs={{0,4},{2,6},{4,0},{6,2},{8,12},{10,14},{12,8},{14,10},{16,20},{18,... | collective-permute-start | bytes 196616 | tf_op jit(solution)/shard_map/ppermute | solution.py:461
  20.6 1.3 %collective-permute-start.2 = (f32[64,256]{1,0:T(8,128)S(1)}, f32[64,256]{1,0:T(8,128)S(1)}, u32[]{:S(2)}, u32[]{:S(2)}) collective-permute-start(f32[64,256]{1,0:T(8,128)S(1)} %shard_map.87.held_ref), channel_id=1, source_target_pairs={{0,1},{1,0},{2,3},{3,2},{4,5},{5,4},{6,7},{7,6},{8,9},{9,8},{10,11... | collective-permute-start | bytes 196616 | tf_op jit(solution)/shard_map/ppermute | solution.py:461
  22.1 4.4 %collective-permute-start.3 = (f32[72,256]{1,0:T(8,128)S(1)}, f32[72,256]{1,0:T(8,128)S(1)}, u32[]{:S(2)}, u32[]{:S(2)}) collective-permute-start(f32[72,256]{1,0:T(8,128)S(1)} %shard_map.88.message_ref), channel_id=1, source_target_pairs={{0,8},{8,0},{16,24},{24,16},{1,9},{9,1},{17,25},{25,17},{2,10},{10... | collective-permute-start | bytes 221192 | tf_op jit(solution)/shard_map/ppermute | solution.py:25
  26.5 4.4 %collective-permute-start.4 = (f32[72,256]{1,0:T(8,128)S(1)}, f32[72,256]{1,0:T(8,128)S(1)}, u32[]{:S(2)}, u32[]{:S(2)}) collective-permute-start(f32[72,256]{1,0:T(8,128)S(1)} %shard_map.89.refs_0_.refs_2_), channel_id=1, source_target_pairs={{0,16},{8,24},{16,0},{24,8},{1,17},{9,25},{17,1},{25,9},{2,18},{10... | collective-permute-start | bytes 221192 | tf_op jit(solution)/shard_map/ppermute | solution.py:25
  27.1 8.2 %collective-permute-start.16 = (f32[32,1536]{1,0:T(8,128)S(1)}, f32[32,1536]{1,0:T(8,128)S(1)}, u32[]{:S(2)}, u32[]{:S(2)}) collective-permute-start(f32[32,1536]{1,0:T(8,128)S(1)} %get-tuple-element.44), channel_id=1, source_target_pairs={{0,2},{1,3},{2,0},{3,1},{4,6},{5,7},{6,4},{7,5},{8,10},{9,11},{10,... | collective-permute-start | bytes 589832 | tf_op jit(solution)/shard_map/ppermute | solution.py:25
  31.7 42.6 %collective-permute-start.8 = (f32[64,2688]{1,0:T(8,128)S(1)}, f32[64,2688]{1,0:T(8,128)S(1)}, u32[]{:S(2)}, u32[]{:S(2)}) collective-permute-start(f32[64,2688]{1,0:T(8,128)S(1)} %get-tuple-element.33), channel_id=1, source_target_pairs={{0,16},{8,24},{16,0},{24,8},{1,17},{9,25},{17,1},{25,9},{2,18},{10... | collective-permute-start | bytes 2064392 | tf_op jit(solution)/shard_map/ppermute | solution.py:25
  33.1 42.2 %collective-permute-start.6 = (f32[64,2688]{1,0:T(8,128)S(1)}, f32[64,2688]{1,0:T(8,128)S(1)}, u32[]{:S(2)}, u32[]{:S(2)}) collective-permute-start(f32[64,2688]{1,0:T(8,128)S(1)} %get-tuple-element.30), channel_id=1, source_target_pairs={{0,8},{8,0},{16,24},{24,16},{1,9},{9,1},{17,25},{25,17},{2,10},{10... | collective-permute-start | bytes 2064392 | tf_op jit(solution)/shard_map/ppermute | solution.py:25
  33.5 10.3 %collective-permute-start.12 = (f32[32,1536]{1,0:T(8,128)S(1)}, f32[32,1536]{1,0:T(8,128)S(1)}, u32[]{:S(2)}, u32[]{:S(2)}) collective-permute-start(f32[32,1536]{1,0:T(8,128)S(1)} %get-tuple-element.41), channel_id=1, source_target_pairs={{0,2},{1,3},{2,0},{3,1},{4,6},{5,7},{6,4},{7,5},{8,10},{9,11},{10,... | collective-permute-start | bytes 589832 | tf_op jit(solution)/shard_map/ppermute | solution.py:25
  35.3 16.0 %collective-permute-start.17 = (f32[32,1536]{1,0:T(8,128)S(1)}, f32[32,1536]{1,0:T(8,128)S(1)}, u32[]{:S(2)}, u32[]{:S(2)}) collective-permute-start(f32[32,1536]{1,0:T(8,128)S(1)} %shard_map.98.refs_2_), channel_id=1, source_target_pairs={{0,4},{1,5},{2,6},{3,7},{4,0},{5,1},{6,2},{7,3},{8,12},{9,13},{10,... | collective-permute-start | bytes 589832 | tf_op jit(solution)/shard_map/ppermute | solution.py:25
  38.5 12.8 %collective-permute-start.15 = (f32[32,1024]{1,0:T(8,128)S(1)}, f32[32,1024]{1,0:T(8,128)S(1)}, u32[]{:S(2)}, u32[]{:S(2)}) collective-permute-start(f32[32,1024]{1,0:T(8,128)S(1)} %get-tuple-element.42.refs_0_), channel_id=1, source_target_pairs={{0,4},{1,5},{2,6},{3,7},{4,0},{5,1},{6,2},{7,3},{8,12},{9,13},{10,... | collective-permute-start | bytes 393224 | tf_op jit(solution)/shard_map/ppermute | solution.py:25
  43.8 12.5 %collective-permute-start.9 = (f32[32,1024]{1,0:T(8,128)S(1)}, f32[32,1024]{1,0:T(8,128)S(1)}, u32[]{:S(2)}, u32[]{:S(2)}) collective-permute-start(f32[32,1024]{1,0:T(8,128)S(1)} %get-tuple-element.39), channel_id=1, source_target_pairs={{0,2},{1,3},{2,0},{3,1},{4,6},{5,7},{6,4},{7,5},{8,10},{9,11},{10,... | collective-permute-start | bytes 393224 | tf_op jit(solution)/shard_map/ppermute | solution.py:25
  43.8 26.2 %copy-start.1 = (s32[1,2]{1,0:T(1,128)S(1)}, s32[1,2]{1,0:T(1,128)}, u32[]{:S(2)}) copy-start(s32[1,2]{1,0:T(1,128)} %points_ref.5) | copy-start | bytes 28
  51.3 10.5 %collective-permute-start.13 = (f32[32,1536]{1,0:T(8,128)S(1)}, f32[32,1536]{1,0:T(8,128)S(1)}, u32[]{:S(2)}, u32[]{:S(2)}) collective-permute-start(f32[32,1536]{1,0:T(8,128)S(1)} %shard_map.96.refs_0_), channel_id=1, source_target_pairs={{0,4},{1,5},{2,6},{3,7},{4,0},{5,1},{6,2},{7,3},{8,12},{9,13},{10,... | collective-permute-start | bytes 589832 | tf_op jit(solution)/shard_map/ppermute | solution.py:25
  51.3 18.7 %collective-permute-start.18 = (f32[32,2560]{1,0:T(8,128)S(1)}, f32[32,2560]{1,0:T(8,128)S(1)}, u32[]{:S(2)}, u32[]{:S(2)}) collective-permute-start(f32[32,2560]{1,0:T(8,128)S(1)} %shard_map.99.piece_ref), channel_id=1, source_target_pairs={{0,2},{1,3},{2,0},{3,1},{4,6},{5,7},{6,4},{7,5},{8,10},{9,11},{10,... | collective-permute-start | bytes 983048 | tf_op jit(solution)/shard_map/ppermute | solution.py:25
  56.3 10.6 %collective-permute-start.10 = (f32[32,1024]{1,0:T(8,128)S(1)}, f32[32,1024]{1,0:T(8,128)S(1)}, u32[]{:S(2)}, u32[]{:S(2)}) collective-permute-start(f32[32,1024]{1,0:T(8,128)S(1)} %shard_map.94.refs_0_), channel_id=1, source_target_pairs={{0,4},{1,5},{2,6},{3,7},{4,0},{5,1},{6,2},{7,3},{8,12},{9,13},{10,... | collective-permute-start | bytes 393224 | tf_op jit(solution)/shard_map/ppermute | solution.py:25
  61.8 9.7 %collective-permute-start.14 = (f32[32,1536]{1,0:T(8,128)S(1)}, f32[32,1536]{1,0:T(8,128)S(1)}, u32[]{:S(2)}, u32[]{:S(2)}) collective-permute-start(f32[32,1536]{1,0:T(8,128)S(1)} %shard_map.97.piece_ref), channel_id=1, source_target_pairs={{0,2},{1,3},{2,0},{3,1},{4,6},{5,7},{6,4},{7,5},{8,10},{9,11},{10,... | collective-permute-start | bytes 589832 | tf_op jit(solution)/shard_map/ppermute | solution.py:25
  66.9 6.1 %collective-permute-start.11 = (f32[32,1024]{1,0:T(8,128)S(1)}, f32[32,1024]{1,0:T(8,128)S(1)}, u32[]{:S(2)}, u32[]{:S(2)}) collective-permute-start(f32[32,1024]{1,0:T(8,128)S(1)} %shard_map.95.piece_ref), channel_id=1, source_target_pairs={{0,2},{1,3},{2,0},{3,1},{4,6},{5,7},{6,4},{7,5},{8,10},{9,11},{10,... | collective-permute-start | bytes 393224 | tf_op jit(solution)/shard_map/ppermute | solution.py:25
  72.9 1.4 %copy-start = (f32[2,5120]{1,0:T(2,128)S(1)}, f32[2,5120]{1,0:T(2,128)}, u32[]{:S(2)}) copy-start(f32[2,5120]{1,0:T(2,128)} %checksum_ref.3) | copy-start | bytes 122884

commit v3 on v2

--- a/solution.py
+++ b/solution.py
@@ -74,7 +74,7 @@
     half = cols // 2
     deep = rows // 2
     count = len(cuts) - 1
-    pieces = 2
+    pieces = 1
     step = deep // pieces
 
     def kernel(matrix_ref, scale_ref, *refs):
@@ -94,10 +94,10 @@
             copy.start()
         scale = scale_ref[0, 0]
         upper = lax.axis_index("col") // groups & 1
-        for copy in copies:
-            copy.wait()
-        for number in range(count):
-            for side in range(2):
+        for side in range(2):
+            for piece in range(2 * pieces):
+                copies[2 * piece + side].wait()
+            for number in range(count):
                 low = max(cuts[number], side * half)
                 high = min(cuts[number + 1], (side + 1) * half)
                 if low < high:

time: 76.4 us -> 76.2 us (level)
  no operation moved by 1% of the time
where the time goes in v3:
time: 76.2 us; the launch traced here: 76 us
  waiting for transfers between devices  37.5 us (49%)
  starting transfers between devices  27.8 us (36%)
  Pallas kernels  9.19 us (12%)
  between operations  1.49 us (2%)
    ppermute x17, waiting for transfers between devices, swap(): lax.ppermute(value, axis, [(i, i ^ mask) for i in range(lax.axis_size(axi...  33.7 us
    ppermute x17, starting transfers between devices, swap(): lax.ppermute(value, axis, [(i, i ^ mask) for i in range(lax.axis_size(axi...  23.2 us
    pallas_call x18, Pallas kernels, call(): pl.pallas_call(kernel, out_shape=outs, in_specs=in_specs, out_specs=place...  9.19 us
    ppermute x2, starting transfers between devices, per_device(): came.append(lax.ppermute(lower, 'col', route))  4.57 us
    ppermute x2, waiting for transfers between devices, per_device(): came.append(lax.ppermute(lower, 'col', route))  3.79 us
  transfers between devices with their start and end apart: 19, of which 10 were waited for; matrix products, arithmetic and copies ran while one was open for 0% of the time, Pallas kernels for 9%

profile of v3, /device:TPU:0, one launch (start us, length us, event | category | flops | bytes accessed | tf_op | source)
XLA Modules:
  0.0 76.0 jit_solution(8775226860868532685)
XLA Ops:
  1.3 1.4 %shard_map.85 = (f32[64,2560]{1,0:T(8,128)S(1)}, f32[64,2560]{1,0:T(8,128)S(1)}, f32[64,256]{1,0:T(8,128)S(1)}, f32[32,1536]{1,0:T(8,128)S(1)}, f32[32,1024]{1,0...) custom-call(f32[64,5120]{1,0:T(8,128)} %matrix_ref.1, ...), custom_call_target="tpu_custom_call" | custom-call | tf_op jit(solution)/shard_map/pallas_call | solution.py:60
  2.7 3.0 %collective-permute-start.7 = (f32[64,2560]{1,0:T(8,128)S(1)}, f32[64,2560]{1,0:T(8,128)S(1)}, u32[]{:S(2)}, u32[]{:S(2)}) collective-permute-start(f32[64,2560]{1,0:T(8,128)S(1)} %get-tuple-element.31.refs_4_.matrix_ref), channel_id=1, source_target_pairs={{0,8},{8,0},{16,24},{24,16},{1,9},{9,1},{17,25},{25,17},{2,10},{10... | collective-permute-start | bytes 1966088 | tf_op jit(solution)/shard_map/ppermute | solution.py:25
  5.7 1.5 %collective-permute-start.5 = (f32[64,2560]{1,0:T(8,128)S(1)}, f32[64,2560]{1,0:T(8,128)S(1)}, u32[]{:S(2)}, u32[]{:S(2)}) collective-permute-start(f32[64,2560]{1,0:T(8,128)S(1)} %get-tuple-element.24.refs_4_.matrix_ref), channel_id=1, source_target_pairs={{0,16},{8,24},{16,0},{24,8},{1,17},{9,25},{17,1},{25,9},{2,18},{10... | collective-permute-start | bytes 1966088 | tf_op jit(solution)/shard_map/ppermute | solution.py:25
  7.2 1.6 %collective-permute-start = (f32[32,1536]{1,0:T(8,128)S(1)}, f32[32,1536]{1,0:T(8,128)S(1)}, u32[]{:S(2)}, u32[]{:S(2)}) collective-permute-start(f32[32,1536]{1,0:T(8,128)S(1)} %get-tuple-element.26), channel_id=1, source_target_pairs={{0,2},{1,3},{2,0},{3,1},{4,6},{5,7},{6,4},{7,5},{8,10},{9,11},{10,... | collective-permute-start | bytes 589832 | tf_op jit(solution)/shard_map/ppermute | solution.py:25
  8.8 4.5 %collective-permute-done.arrived_ref = f32[32,1536]{1,0:T(8,128)S(1)} collective-permute-done((f32[32,1536]{1,0:T(8,128)S(1)}, f32[32,1536]{1,0:T(8,128)S(1)}, u32[]{:S(2)}, u32[]{:S(2)}) %collective-permute-start) | collective-permute-done | bytes 196640 | tf_op jit(solution)/shard_map/ppermute | solution.py:25
  13.3 4.5 %collective-permute-start.1 = (f32[64,256]{1,0:T(8,128)S(1)}, f32[64,256]{1,0:T(8,128)S(1)}, u32[]{:S(2)}, u32[]{:S(2)}) collective-permute-start(f32[64,256]{1,0:T(8,128)S(1)} %get-tuple-element.28.held_ref), channel_id=1, source_target_pairs={{0,4},{2,6},{4,0},{6,2},{8,12},{10,14},{12,8},{14,10},{16,20},{18,... | collective-permute-start | bytes 196616 | tf_op jit(solution)/shard_map/ppermute | solution.py:461
  17.8 2.6 %collective-permute-done.1.refs_0_ = f32[64,256]{1,0:T(8,128)S(1)} collective-permute-done((f32[64,256]{1,0:T(8,128)S(1)}, f32[64,256]{1,0:T(8,128)S(1)}, u32[]{:S(2)}, u32[]{:S(2)}) %collective-permute-start.1) | collective-permute-done | bytes 65568 | tf_op jit(solution)/shard_map/ppermute | solution.py:461
  20.5 1.2 %collective-permute-done.2.refs_0_ = f32[64,256]{1,0:T(8,128)S(1)} collective-permute-done((f32[64,256]{1,0:T(8,128)S(1)}, f32[64,256]{1,0:T(8,128)S(1)}, u32[]{:S(2)}, u32[]{:S(2)}) %collective-permute-start.2) | collective-permute-done | bytes 65568 | tf_op jit(solution)/shard_map/ppermute | solution.py:461
  21.7 0.2 shard_map.88.message_ref
  21.9 0.5 collective-permute-start.3
  22.5 3.8 %collective-permute-done.3.refs_0_.refs_1_ = f32[72,256]{1,0:T(8,128)S(1)} collective-permute-done((f32[72,256]{1,0:T(8,128)S(1)}, f32[72,256]{1,0:T(8,128)S(1)}, u32[]{:S(2)}, u32[]{:S(2)}) %collective-permute-start.3) | collective-permute-done | bytes 73760 | tf_op jit(solution)/shard_map/ppermute | solution.py:25
  26.3 0.6 collective-permute-start.4
  26.9 1.6 %collective-permute-start.16 = (f32[32,1536]{1,0:T(8,128)S(1)}, f32[32,1536]{1,0:T(8,128)S(1)}, u32[]{:S(2)}, u32[]{:S(2)}) collective-permute-start(f32[32,1536]{1,0:T(8,128)S(1)} %get-tuple-element.44), channel_id=1, source_target_pairs={{0,2},{1,3},{2,0},{3,1},{4,6},{5,7},{6,4},{7,5},{8,10},{9,11},{10,... | collective-permute-start | bytes 589832 | tf_op jit(solution)/shard_map/ppermute | solution.py:25
  28.5 2.3 %collective-permute-done.4.refs_3_.refs_1_ = f32[72,256]{1,0:T(8,128)S(1)} collective-permute-done((f32[72,256]{1,0:T(8,128)S(1)}, f32[72,256]{1,0:T(8,128)S(1)}, u32[]{:S(2)}, u32[]{:S(2)}) %collective-permute-start.4) | collective-permute-done | bytes 73760 | tf_op jit(solution)/shard_map/ppermute | solution.py:25
  30.7 0.8 %shard_map.91 = (f32[64,2688]{1,0:T(8,128)S(1)}, f32[64,2688]{1,0:T(8,128)S(1)}) custom-call(s32[1,256]{1,0:T(1,128)S(1)} %bitcast.1, f32[72,256]{1,0:T(8,128)S(1)} %shard_map.89.refs_0_.refs_2_, f32[72,256]{1,0:T(8,128)S(1)} %collective-permute-done.4.refs_3_.refs_1_, f32[72,256]{1,0:T(8,128)S(1)} %shard_map.89.refs_0_.refs_2_, ...), custom_call_target="tpu_custom_call" | custom-call | flops 89128960 | tf_op jit(solution)/shard_map/pallas_call | solution.py:60
  31.5 0.6 collective-permute-start.8
  32.1 0.8 %shard_map.90 = (f32[64,2688]{1,0:T(8,128)S(1)}, f32[64,2688]{1,0:T(8,128)S(1)}) custom-call(s32[1,256]{1,0:T(1,128)S(1)} %bitcast.2, f32[72,256]{1,0:T(8,128)S(1)} %shard_map.89.refs_0_.refs_2_, f32[72,256]{1,0:T(8,128)S(1)} %collective-permute-done.3.refs_0_.refs_1_, f32[72,256]{1,0:T(8,128)S(1)} %shard_map.89.refs_0_.refs_2_, ...), custom_call_target="tpu_custom_call" | custom-call | flops 89128960 | tf_op jit(solution)/shard_map/pallas_call | solution.py:60
  32.9 0.4 collective-permute-start.6
  33.3 1.7 %collective-permute-start.12 = (f32[32,1536]{1,0:T(8,128)S(1)}, f32[32,1536]{1,0:T(8,128)S(1)}, u32[]{:S(2)}, u32[]{:S(2)}) collective-permute-start(f32[32,1536]{1,0:T(8,128)S(1)} %get-tuple-element.41), channel_id=1, source_target_pairs={{0,2},{1,3},{2,0},{3,1},{4,6},{5,7},{6,4},{7,5},{8,10},{9,11},{10,... | collective-permute-start | bytes 589832 | tf_op jit(solution)/shard_map/ppermute | solution.py:25
  35.1 3.2 %collective-permute-start.17 = (f32[32,1536]{1,0:T(8,128)S(1)}, f32[32,1536]{1,0:T(8,128)S(1)}, u32[]{:S(2)}, u32[]{:S(2)}) collective-permute-start(f32[32,1536]{1,0:T(8,128)S(1)} %shard_map.98.refs_2_), channel_id=1, source_target_pairs={{0,4},{1,5},{2,6},{3,7},{4,0},{5,1},{6,2},{7,3},{8,12},{9,13},{10,... | collective-permute-start | bytes 589832 | tf_op jit(solution)/shard_map/ppermute | solution.py:25
  38.4 5.2 %collective-permute-done.12.arrived_ref = f32[32,1536]{1,0:T(8,128)S(1)} collective-permute-done((f32[32,1536]{1,0:T(8,128)S(1)}, f32[32,1536]{1,0:T(8,128)S(1)}, u32[]{:S(2)}, u32[]{:S(2)}) %collective-permute-start.12) | collective-permute-done | bytes 196640 | tf_op jit(solution)/shard_map/ppermute | solution.py:25
  43.6 7.5 %collective-permute-done.15.refs_1_ = f32[32,1024]{1,0:T(8,128)S(1)} collective-permute-done((f32[32,1024]{1,0:T(8,128)S(1)}, f32[32,1024]{1,0:T(8,128)S(1)}, u32[]{:S(2)}, u32[]{:S(2)}) %collective-permute-start.15) | collective-permute-done | bytes 131104 | tf_op jit(solution)/shard_map/ppermute | solution.py:25
  51.1 4.9 %collective-permute-start.18 = (f32[32,2560]{1,0:T(8,128)S(1)}, f32[32,2560]{1,0:T(8,128)S(1)}, u32[]{:S(2)}, u32[]{:S(2)}) collective-permute-start(f32[32,2560]{1,0:T(8,128)S(1)} %shard_map.99.piece_ref), channel_id=1, source_target_pairs={{0,2},{1,3},{2,0},{3,1},{4,6},{5,7},{6,4},{7,5},{8,10},{9,11},{10,... | collective-permute-start | bytes 983048 | tf_op jit(solution)/shard_map/ppermute | solution.py:25
  56.2 5.5 %collective-permute-done.13.refs_1_ = f32[32,1536]{1,0:T(8,128)S(1)} collective-permute-done((f32[32,1536]{1,0:T(8,128)S(1)}, f32[32,1536]{1,0:T(8,128)S(1)}, u32[]{:S(2)}, u32[]{:S(2)}) %collective-permute-start.13) | collective-permute-done | bytes 196640 | tf_op jit(solution)/shard_map/ppermute | solution.py:25
  61.6 0.2 collective-permute-start.14
  61.8 4.8 %collective-permute-done.10.refs_1_ = f32[32,1024]{1,0:T(8,128)S(1)} collective-permute-done((f32[32,1024]{1,0:T(8,128)S(1)}, f32[32,1024]{1,0:T(8,128)S(1)}, u32[]{:S(2)}, u32[]{:S(2)}) %collective-permute-start.10) | collective-permute-done | bytes 131104 | tf_op jit(solution)/shard_map/ppermute | solution.py:25
  66.7 3.2 %collective-permute-start.11 = (f32[32,1024]{1,0:T(8,128)S(1)}, f32[32,1024]{1,0:T(8,128)S(1)}, u32[]{:S(2)}, u32[]{:S(2)}) collective-permute-start(f32[32,1024]{1,0:T(8,128)S(1)} %shard_map.95.piece_ref), channel_id=1, source_target_pairs={{0,2},{1,3},{2,0},{3,1},{4,6},{5,7},{6,4},{7,5},{8,10},{9,11},{10,... | collective-permute-start | bytes 393224 | tf_op jit(solution)/shard_map/ppermute | solution.py:25
  69.9 1.5 %shard_map.100.refs_0_ = f32[64,5120]{1,0:T(8,128)} custom-call(s32[1,2]{1,0:T(1,128)S(1)} %copy-done.1, f32[32,2560]{1,0:T(8,128)S(1)} %shard_map.99.piece_ref, f32[32,2560]{1,0:T(8,128)S(1)} %collective-permute-done.18.arrived_ref), custom_call_target="tpu_custom_call" | custom-call | tf_op jit(solution)/shard_map/pallas_call | solution.py:60
  71.3 1.3 %shard_map.101.refs_0_ = f32[64,5120]{1,0:T(8,128)} custom-call(s32[1,2]{1,0:T(1,128)S(1)} %copy-done.1, f32[32,1536]{1,0:T(8,128)S(1)} %shard_map.97.piece_ref, f32[32,1536]{1,0:T(8,128)S(1)} %collective-permute-done.14.arrived_ref, f32[64,5120]{1,0:T(8,128)} %shard_map.100.refs_0_), custom_call_target="tpu_custom_call", output_to_operand_aliasing={{}: (3, {})} | custom-call | tf_op jit(solution)/shard_map/pallas_call | solution.py:60
  72.8 1.3 %shard_map.102 = f32[64,5120]{1,0:T(8,128)} custom-call(s32[1,2]{1,0:T(1,128)S(1)} %copy-done.1, f32[32,1024]{1,0:T(8,128)S(1)} %shard_map.95.piece_ref, f32[32,1024]{1,0:T(8,128)S(1)} %collective-permute-done.11.arrived_ref, f32[64,5120]{1,0:T(8,128)} %shard_map.101.refs_0_), custom_call_target="tpu_custom_call", output_to_operand_aliasing={{}: (3, {})} | custom-call | tf_op jit(solution)/shard_map/pallas_call | solution.py:60
  74.1 0.9 %shard_map.92 = (f32[64,5120]{1,0:T(8,128)}, f32[2,5120]{1,0:T(2,128)}) custom-call(f32[64,2560]{1,0:T(8,128)S(1)} %get-tuple-element.31.refs_4_.matrix_ref, f32[2,5120]{1,0:T(2,128)S(1)} %copy-done, f32[64,2688]{1,0:T(8,128)S(1)} %get-tuple-element.32.kept_ref, f32[64,2688]{1,0:T(8,128)S(1)} %collective-permute-done.8.arrived_ref), custom_call_target="tpu_custom_call" | custom-call | tf_op jit(solution)/shard_map/pallas_call | solution.py:60
  75.1 0.9 %shard_map.93 = (f32[64,5120]{1,0:T(8,128)}, f32[2,5120]{1,0:T(2,128)}) custom-call(f32[64,2560]{1,0:T(8,128)S(1)} %get-tuple-element.24.refs_4_.matrix_ref, f32[2,5120]{1,0:T(2,128)S(1)} %copy-done, f32[64,2688]{1,0:T(8,128)S(1)} %get-tuple-element.29.kept_ref, ...), custom_call_target="tpu_custom_call", output_to_operand_aliasing={{0}: (4, {}), {1}: (5, {})} | custom-call | tf_op jit(solution)/shard_map/pallas_call | solution.py:60
  (32 shorter events, 0.6 us)
Async XLA Ops:
  0.6 21.1 %copy-start.3 = (f32[2,64]{1,0:T(2,128)S(1)}, f32[2,64]{1,0:T(2,128)}, u32[]{:S(2)}) copy-start(f32[2,64]{1,0:T(2,128)} %weights_ref.1) | copy-start | bytes 1540
  0.6 30.1 %copy-start.2 = (s32[256]{0:T(256)S(1)}, s32[256]{0:T(256)}, u32[]{:S(2)}) copy-start(s32[256]{0:T(256)} %param.7) | copy-start | bytes 3076
  2.7 28.0 %collective-permute-start.7 = (f32[64,2560]{1,0:T(8,128)S(1)}, f32[64,2560]{1,0:T(8,128)S(1)}, u32[]{:S(2)}, u32[]{:S(2)}) collective-permute-start(f32[64,2560]{1,0:T(8,128)S(1)} %get-tuple-element.31.refs_4_.matrix_ref), channel_id=1, source_target_pairs={{0,8},{8,0},{16,24},{24,16},{1,9},{9,1},{17,25},{25,17},{2,10},{10... | collective-permute-start | bytes 1966088 | tf_op jit(solution)/shard_map/ppermute | solution.py:25
  5.7 26.4 %collective-permute-start.5 = (f32[64,2560]{1,0:T(8,128)S(1)}, f32[64,2560]{1,0:T(8,128)S(1)}, u32[]{:S(2)}, u32[]{:S(2)}) collective-permute-start(f32[64,2560]{1,0:T(8,128)S(1)} %get-tuple-element.24.refs_4_.matrix_ref), channel_id=1, source_target_pairs={{0,16},{8,24},{16,0},{24,8},{1,17},{9,25},{17,1},{25,9},{2,18},{10... | collective-permute-start | bytes 1966088 | tf_op jit(solution)/shard_map/ppermute | solution.py:25
  7.2 6.1 %collective-permute-start = (f32[32,1536]{1,0:T(8,128)S(1)}, f32[32,1536]{1,0:T(8,128)S(1)}, u32[]{:S(2)}, u32[]{:S(2)}) collective-permute-start(f32[32,1536]{1,0:T(8,128)S(1)} %get-tuple-element.26), channel_id=1, source_target_pairs={{0,2},{1,3},{2,0},{3,1},{4,6},{5,7},{6,4},{7,5},{8,10},{9,11},{10,... | collective-permute-start | bytes 589832 | tf_op jit(solution)/shard_map/ppermute | solution.py:25
  13.3 7.1 %collective-permute-start.1 = (f32[64,256]{1,0:T(8,128)S(1)}, f32[64,256]{1,0:T(8,128)S(1)}, u32[]{:S(2)}, u32[]{:S(2)}) collective-permute-start(f32[64,256]{1,0:T(8,128)S(1)} %get-tuple-element.28.held_ref), channel_id=1, source_target_pairs={{0,4},{2,6},{4,0},{6,2},{8,12},{10,14},{12,8},{14,10},{16,20},{18,... | collective-permute-start | bytes 196616 | tf_op jit(solution)/shard_map/ppermute | solution.py:461
  20.4 1.3 %collective-permute-start.2 = (f32[64,256]{1,0:T(8,128)S(1)}, f32[64,256]{1,0:T(8,128)S(1)}, u32[]{:S(2)}, u32[]{:S(2)}) collective-permute-start(f32[64,256]{1,0:T(8,128)S(1)} %shard_map.87.held_ref), channel_id=1, source_target_pairs={{0,1},{1,0},{2,3},{3,2},{4,5},{5,4},{6,7},{7,6},{8,9},{9,8},{10,11... | collective-permute-start | bytes 196616 | tf_op jit(solution)/shard_map/ppermute | solution.py:461
  21.9 4.4 %collective-permute-start.3 = (f32[72,256]{1,0:T(8,128)S(1)}, f32[72,256]{1,0:T(8,128)S(1)}, u32[]{:S(2)}, u32[]{:S(2)}) collective-permute-start(f32[72,256]{1,0:T(8,128)S(1)} %shard_map.88.message_ref), channel_id=1, source_target_pairs={{0,8},{8,0},{16,24},{24,16},{1,9},{9,1},{17,25},{25,17},{2,10},{10... | collective-permute-start | bytes 221192 | tf_op jit(solution)/shard_map/ppermute | solution.py:25
  26.3 4.4 %collective-permute-start.4 = (f32[72,256]{1,0:T(8,128)S(1)}, f32[72,256]{1,0:T(8,128)S(1)}, u32[]{:S(2)}, u32[]{:S(2)}) collective-permute-start(f32[72,256]{1,0:T(8,128)S(1)} %shard_map.89.refs_0_.refs_2_), channel_id=1, source_target_pairs={{0,16},{8,24},{16,0},{24,8},{1,17},{9,25},{17,1},{25,9},{2,18},{10... | collective-permute-start | bytes 221192 | tf_op jit(solution)/shard_map/ppermute | solution.py:25
  26.9 8.2 %collective-permute-start.16 = (f32[32,1536]{1,0:T(8,128)S(1)}, f32[32,1536]{1,0:T(8,128)S(1)}, u32[]{:S(2)}, u32[]{:S(2)}) collective-permute-start(f32[32,1536]{1,0:T(8,128)S(1)} %get-tuple-element.44), channel_id=1, source_target_pairs={{0,2},{1,3},{2,0},{3,1},{4,6},{5,7},{6,4},{7,5},{8,10},{9,11},{10,... | collective-permute-start | bytes 589832 | tf_op jit(solution)/shard_map/ppermute | solution.py:25
  31.5 42.6 %collective-permute-start.8 = (f32[64,2688]{1,0:T(8,128)S(1)}, f32[64,2688]{1,0:T(8,128)S(1)}, u32[]{:S(2)}, u32[]{:S(2)}) collective-permute-start(f32[64,2688]{1,0:T(8,128)S(1)} %get-tuple-element.33), channel_id=1, source_target_pairs={{0,16},{8,24},{16,0},{24,8},{1,17},{9,25},{17,1},{25,9},{2,18},{10... | collective-permute-start | bytes 2064392 | tf_op jit(solution)/shard_map/ppermute | solution.py:25
  32.9 42.2 %collective-permute-start.6 = (f32[64,2688]{1,0:T(8,128)S(1)}, f32[64,2688]{1,0:T(8,128)S(1)}, u32[]{:S(2)}, u32[]{:S(2)}) collective-permute-start(f32[64,2688]{1,0:T(8,128)S(1)} %get-tuple-element.30), channel_id=1, source_target_pairs={{0,8},{8,0},{16,24},{24,16},{1,9},{9,1},{17,25},{25,17},{2,10},{10... | collective-permute-start | bytes 2064392 | tf_op jit(solution)/shard_map/ppermute | solution.py:25
  33.3 10.3 %collective-permute-start.12 = (f32[32,1536]{1,0:T(8,128)S(1)}, f32[32,1536]{1,0:T(8,128)S(1)}, u32[]{:S(2)}, u32[]{:S(2)}) collective-permute-start(f32[32,1536]{1,0:T(8,128)S(1)} %get-tuple-element.41), channel_id=1, source_target_pairs={{0,2},{1,3},{2,0},{3,1},{4,6},{5,7},{6,4},{7,5},{8,10},{9,11},{10,... | collective-permute-start | bytes 589832 | tf_op jit(solution)/shard_map/ppermute | solution.py:25
  35.1 16.0 %collective-permute-start.17 = (f32[32,1536]{1,0:T(8,128)S(1)}, f32[32,1536]{1,0:T(8,128)S(1)}, u32[]{:S(2)}, u32[]{:S(2)}) collective-permute-start(f32[32,1536]{1,0:T(8,128)S(1)} %shard_map.98.refs_2_), channel_id=1, source_target_pairs={{0,4},{1,5},{2,6},{3,7},{4,0},{5,1},{6,2},{7,3},{8,12},{9,13},{10,... | collective-permute-start | bytes 589832 | tf_op jit(solution)/shard_map/ppermute | solution.py:25
  38.3 12.8 %collective-permute-start.15 = (f32[32,1024]{1,0:T(8,128)S(1)}, f32[32,1024]{1,0:T(8,128)S(1)}, u32[]{:S(2)}, u32[]{:S(2)}) collective-permute-start(f32[32,1024]{1,0:T(8,128)S(1)} %get-tuple-element.42.refs_0_), channel_id=1, source_target_pairs={{0,4},{1,5},{2,6},{3,7},{4,0},{5,1},{6,2},{7,3},{8,12},{9,13},{10,... | collective-permute-start | bytes 393224 | tf_op jit(solution)/shard_map/ppermute | solution.py:25
  43.6 12.5 %collective-permute-start.9 = (f32[32,1024]{1,0:T(8,128)S(1)}, f32[32,1024]{1,0:T(8,128)S(1)}, u32[]{:S(2)}, u32[]{:S(2)}) collective-permute-start(f32[32,1024]{1,0:T(8,128)S(1)} %get-tuple-element.39), channel_id=1, source_target_pairs={{0,2},{1,3},{2,0},{3,1},{4,6},{5,7},{6,4},{7,5},{8,10},{9,11},{10,... | collective-permute-start | bytes 393224 | tf_op jit(solution)/shard_map/ppermute | solution.py:25
  43.6 26.3 %copy-start.1 = (s32[1,2]{1,0:T(1,128)S(1)}, s32[1,2]{1,0:T(1,128)}, u32[]{:S(2)}) copy-start(s32[1,2]{1,0:T(1,128)} %points_ref.5) | copy-start | bytes 28
  51.1 10.5 %collective-permute-start.13 = (f32[32,1536]{1,0:T(8,128)S(1)}, f32[32,1536]{1,0:T(8,128)S(1)}, u32[]{:S(2)}, u32[]{:S(2)}) collective-permute-start(f32[32,1536]{1,0:T(8,128)S(1)} %shard_map.96.refs_0_), channel_id=1, source_target_pairs={{0,4},{1,5},{2,6},{3,7},{4,0},{5,1},{6,2},{7,3},{8,12},{9,13},{10,... | collective-permute-start | bytes 589832 | tf_op jit(solution)/shard_map/ppermute | solution.py:25
  51.1 18.7 %collective-permute-start.18 = (f32[32,2560]{1,0:T(8,128)S(1)}, f32[32,2560]{1,0:T(8,128)S(1)}, u32[]{:S(2)}, u32[]{:S(2)}) collective-permute-start(f32[32,2560]{1,0:T(8,128)S(1)} %shard_map.99.piece_ref), channel_id=1, source_target_pairs={{0,2},{1,3},{2,0},{3,1},{4,6},{5,7},{6,4},{7,5},{8,10},{9,11},{10,... | collective-permute-start | bytes 983048 | tf_op jit(solution)/shard_map/ppermute | solution.py:25
  56.1 10.6 %collective-permute-start.10 = (f32[32,1024]{1,0:T(8,128)S(1)}, f32[32,1024]{1,0:T(8,128)S(1)}, u32[]{:S(2)}, u32[]{:S(2)}) collective-permute-start(f32[32,1024]{1,0:T(8,128)S(1)} %shard_map.94.refs_0_), channel_id=1, source_target_pairs={{0,4},{1,5},{2,6},{3,7},{4,0},{5,1},{6,2},{7,3},{8,12},{9,13},{10,... | collective-permute-start | bytes 393224 | tf_op jit(solution)/shard_map/ppermute | solution.py:25
  61.6 9.7 %collective-permute-start.14 = (f32[32,1536]{1,0:T(8,128)S(1)}, f32[32,1536]{1,0:T(8,128)S(1)}, u32[]{:S(2)}, u32[]{:S(2)}) collective-permute-start(f32[32,1536]{1,0:T(8,128)S(1)} %shard_map.97.piece_ref), channel_id=1, source_target_pairs={{0,2},{1,3},{2,0},{3,1},{4,6},{5,7},{6,4},{7,5},{8,10},{9,11},{10,... | collective-permute-start | bytes 589832 | tf_op jit(solution)/shard_map/ppermute | solution.py:25
  66.7 6.1 %collective-permute-start.11 = (f32[32,1024]{1,0:T(8,128)S(1)}, f32[32,1024]{1,0:T(8,128)S(1)}, u32[]{:S(2)}, u32[]{:S(2)}) collective-permute-start(f32[32,1024]{1,0:T(8,128)S(1)} %shard_map.95.piece_ref), channel_id=1, source_target_pairs={{0,2},{1,3},{2,0},{3,1},{4,6},{5,7},{6,4},{7,5},{8,10},{9,11},{10,... | collective-permute-start | bytes 393224 | tf_op jit(solution)/shard_map/ppermute | solution.py:25
  72.7 1.4 %copy-start = (f32[2,5120]{1,0:T(2,128)S(1)}, f32[2,5120]{1,0:T(2,128)}, u32[]{:S(2)}) copy-start(f32[2,5120]{1,0:T(2,128)} %checksum_ref.3) | copy-start | bytes 122884
